TPU v7x, 128 devices: a whole 4x4x4 slice. The times are simulated.
128 devices in a mesh: orb: 16 (over z, x), comp: 8 (over y, core).
Axes of the slice: x: 4, y: 4, z: 4, core: 2. Of those that a mesh axis runs over, the one named last changes fastest.
Arguments:
- psi: bfloat16 [1024, 4, 128, 256], P('orb', None, 'comp'), may hold values from -16 to 16
- region_start: int32 [1024], replicated, may hold values from 0 to 63
- region_len: int32 [1024], replicated, may hold values from 32 to 64
- fine_mask: int32 [128, 16], P('comp'), may hold values 0 or 1
- occupation: int32 [1024], replicated, may hold values from 0 to 2
- kinetic_taps: bfloat16 [29, 4, 4], replicated, may hold values from -0.5 to 0.5
- magic_taps: bfloat16 [16, 4], replicated, may hold values from -0.75 to 0.75
- external: float32 [128, 256], P('comp'), may hold values from -12 to 12
Outputs:
- density: float32 [128, 256], P('comp', 'orb')
- psi_next: bfloat16 [1024, 4, 128, 256], P(None, None, 'comp', 'orb')
Inputs may be any that keep to these rules, and one draw needn't show every extreme that they name: region_start + region_len <= 128.
All inputs are finite; a program needn't handle non-finite values. No bound on the sum of `fine_mask` on one device may be relied on, other than what follows from the above.
Results may differ from a plain program's by a relative error of at most 0.012.
Values may be sent and summed in bfloat16 or wider, within the bound.
A program may use at most 128 MiB of HBM per device.

v0:
```python
import jax
import jax.numpy as jnp
from jax import lax
from jax.sharding import PartitionSpec as P

ZB = 16


xc_factor = 0.98474502
step_length = 0.1


def padded(x, sides, width):
    edges = {}
    for axis, dim in sides:
        count, length = (lax.axis_size(axis), x.shape[dim])
        up = [(i, (i + 1) % count) for i in range(count - 1)]
        last = lax.slice_in_dim(x, length - width, length, axis=dim)
        first = lax.slice_in_dim(x, 0, width, axis=dim)
        edges[dim] = (
            lax.ppermute(last, axis, up),
            lax.ppermute(first, axis, [(b, a) for a, b in up]),
        )
    done = []
    for _, dim in sides:
        low, high = edges[dim]
        around = [(width, width) if d in done else (0, 0) for d in range(x.ndim)]
        x = jnp.concatenate([jnp.pad(low, around), x, jnp.pad(high, around)], axis=dim)
        done.append(dim)
    return x


def extended(cells, sides, width):
    for axis, dim in sides:
        count = lax.axis_size(axis)
        ends = count - 1
        head = lax.slice_in_dim(cells, 0, width, axis=dim)
        tail = lax.slice_in_dim(cells, cells.shape[dim] - width, cells.shape[dim], axis=dim)
        cells = jnp.concatenate(
            [
                lax.ppermute(tail, axis, [(i, (i + 1) % count) for i in range(ends)]),
                cells,
                lax.ppermute(head, axis, [((i + 1) % count, i) for i in range(ends)]),
            ],
            axis=dim,
        )
    return cells


def packed_total(arrays, axis):
    line, at, gathered = (jnp.concatenate([a.reshape(-1) for a in arrays]), 0, [])
    subtotal = lax.psum(line, axis)
    for a in arrays:
        gathered.append(subtotal[at : at + a.size].reshape(a.shape))
        at += a.size
    return tuple(gathered)


def onehot_band(window, length, shift, sign, count):
    offset = sign * (jnp.arange(window)[:, None] - jnp.arange(length)[None, :]) + shift
    return (offset[:, :, None] == jnp.arange(count)[None, None, :]).astype(jnp.bfloat16)


def kinetic_kernel(filter_taps, window, length):
    onehot = onehot_band(window, length, 0, 1, filter_taps.shape[0])
    return jnp.einsum(
        "jit,ted->djei", onehot, filter_taps, preferred_element_type=jnp.float32
    ).astype(jnp.bfloat16)


def magic_kernel(magic, window, length):
    onehot = onehot_band(window, length, -7, 1, magic.shape[0])
    return jnp.einsum("jit,td->dji", onehot, magic, preferred_element_type=jnp.float32).astype(
        jnp.bfloat16
    )


def adjoint_kernel(magic, window, length):
    onehot = onehot_band(window, length, 21, -1, magic.shape[0])
    return jnp.einsum("jit,te->jei", onehot, magic, preferred_element_type=jnp.float32).astype(
        jnp.bfloat16
    )


def region_support(starts, lengths, first_plane, slab_len, fine_cells, channels):
    planes = first_plane + jnp.arange(slab_len)
    inside = (planes[None, :] >= starts[:, None]) & (planes[None, :] < (starts + lengths)[:, None])
    channel_on = (jnp.arange(channels)[:, None, None] == 0) | (fine_cells[None] > 0)
    return inside[:, None, :, None] & channel_on[None]


def plane_conv(plane_window, filter_taps, slab_len):
    kernel = kinetic_kernel(filter_taps, plane_window.shape[2], slab_len)
    return jnp.einsum("odjz,djei->oeiz", plane_window, kernel, preferred_element_type=jnp.float32)


def depth_apply(depth_window, filter_taps, magic, cells_out):
    window = depth_window.shape[-1]
    block_len = window - 28
    kernel = kinetic_kernel(filter_taps, window, block_len)
    forward = magic_kernel(magic, window, block_len)
    kinetic = jnp.einsum(
        "odxbj,djei->oexbi", depth_window, kernel, preferred_element_type=jnp.float32
    )
    grid_values = jnp.einsum(
        "odxbj,dji->oxbi", depth_window, forward, preferred_element_type=jnp.float32
    )
    shape = depth_window.shape
    return (
        kinetic.reshape(shape[0], shape[1], shape[2], cells_out),
        grid_values.reshape(shape[0], shape[2], cells_out),
    )


def adjoint_apply(value_window, magic, channels, cells_out):
    window = value_window.shape[-1]
    kernel = adjoint_kernel(magic, window, window - 28)
    result = jnp.einsum("oxbj,jei->oexbi", value_window, kernel, preferred_element_type=jnp.float32)
    return result.reshape(value_window.shape[0], channels, value_window.shape[1], cells_out)


def local(psi, region_start, region_len, fine_mask, occupation, kinetic_taps, magic_taps, external):
    orb_dev, channels, slab_len, cells_z = psi.shape
    orb_count = lax.axis_size("orb")
    comp_count = lax.axis_size("comp")
    orbitals = orb_dev * orb_count
    piece_len = cells_z // orb_count
    grid_cells = slab_len * comp_count * cells_z
    first_plane = lax.axis_index("comp") * slab_len
    first_cell = lax.axis_index("orb") * piece_len
    first_orbital = lax.axis_index("orb") * orb_dev
    fine_cells = jnp.repeat(fine_mask, ZB, axis=1)
    starts = lax.dynamic_slice_in_dim(region_start, first_orbital, orb_dev)
    lengths = lax.dynamic_slice_in_dim(region_len, first_orbital, orb_dev)
    support = region_support(starts, lengths, first_plane, slab_len, fine_cells, channels)
    masked = jnp.where(support, psi, jnp.zeros((), psi.dtype))
    masked_t = lax.all_to_all(masked, "orb", split_axis=3, concat_axis=0, tiled=True)
    fine_piece = lax.dynamic_slice_in_dim(fine_cells, first_cell, piece_len, 1)
    support_t = region_support(
        region_start, region_len, first_plane, slab_len, fine_piece, channels
    )
    grid_window = padded(masked_t, (("orb", 3), ("comp", 2)), 14)
    kinetic, grid_values = depth_apply(
        grid_window[:, :, 14 : 14 + slab_len, None, :], kinetic_taps, magic_taps, piece_len
    )
    kinetic = kinetic + plane_conv(
        grid_window[:, :, :, 14 : 14 + piece_len], kinetic_taps, slab_len
    )
    occupied = occupation.astype(jnp.float32)
    density = jnp.sum(occupied[:, None, None] * grid_values * grid_values, axis=0)
    outer = lax.dynamic_slice_in_dim(external, first_cell, piece_len, 1)
    potential = outer - xc_factor * jnp.cbrt(density)
    weighted = (potential[None] * grid_values).astype(jnp.bfloat16)
    value_window = extended(weighted, (("orb", 2),), 14)
    total_applied = kinetic + adjoint_apply(
        value_window[:, :, None, :], magic_taps, channels, piece_len
    )
    applied_t = jnp.where(support_t, total_applied, jnp.zeros((), jnp.float32)).astype(jnp.bfloat16)
    masked_rows = masked_t.reshape(orbitals, -1)
    applied_rows = applied_t.reshape(orbitals, -1)
    intersection_part = jnp.einsum(
        "ik,jk->ij", masked_rows, masked_rows, preferred_element_type=jnp.float32
    )
    lagrange_part = jnp.einsum(
        "ik,jk->ij", applied_rows, masked_rows, preferred_element_type=jnp.float32
    )
    intersection_sum, lagrange_sum = packed_total(
        (intersection_part, lagrange_part), ("orb", "comp")
    )
    intersection_round = (intersection_sum / grid_cells).astype(jnp.bfloat16)
    lagrange_round = (lagrange_sum / grid_cells).astype(jnp.bfloat16)
    gradient = applied_rows.astype(jnp.float32) - jnp.dot(
        lagrange_round, masked_rows, preferred_element_type=jnp.float32
    )
    trial = (masked_rows.astype(jnp.float32) - step_length * gradient).astype(jnp.bfloat16)
    following = 1.5 * trial.astype(jnp.float32) - 0.5 * jnp.dot(
        intersection_round, trial, preferred_element_type=jnp.float32
    )
    psi_next = following.astype(jnp.bfloat16).reshape(orbitals, channels, slab_len, piece_len)
    return (density, psi_next)


def solution(mesh):
    return jax.shard_map(
        local,
        mesh=mesh,
        in_specs=(
            P("orb", None, "comp", None),
            P(),
            P(),
            P("comp", None),
            P(),
            P(),
            P(),
            P("comp", None),
        ),
        out_specs=(P("comp", "orb"), P(None, None, "comp", "orb")),
        check_vma=False,
    )
```

profile of v0, /device:TPU:1, one launch (start us, length us, event | category | flops | bytes accessed | tf_op | source)
XLA Modules:
  0.0 386.6 jit_solution(17336483749501227224)
XLA Ops:
  7.2 0.0 copy-start
  7.2 0.8 broadcast_in_dim.8
  8.0 0.1 broadcast_in_dim_reshape.3
  8.2 0.1 copy.27
  8.3 8.8 %copy.28 = bf16[64,4,16,256]{0,2,1,3:T(8,128)(2,1)} copy(bf16[64,4,16,256]{3,2,1,0:T(8,128)(2,1)} %param.8) | data formatting | bytes 4194304 | tf_op args[0]
  17.1 0.2 broadcast_or_fusion
  17.3 0.1 dynamic-slice_add_fusion
  17.4 0.1 compare_and_fusion.1
  17.5 7.7 %fusion.48 = bf16[256,4,16,64]{3,2,1,0:T(8,128)(2,1)} fusion(bf16[64,4,16,256]{0,2,1,3:T(8,128)(2,1)} %copy.28, pred[4,16,256]{1,0,2:T(4,128)(4,1)S(1)} %broadcast_or_fusion, pred[64,16]{0,1:T(8,128)(4,1)S(1)} %compare_and_fusion.1), kind=kLoop, calls=%fused_computation.81 | loop fusion | flops 2097152 | bytes 4211712
  25.2 7.5 %reshape.243 = bf16[16,2,32768]{2,1,0:T(2,128)(2,1)} reshape(bf16[256,4,16,64]{3,2,1,0:T(8,128)(2,1)} %fusion.48) | data formatting | bytes 4194304
  32.7 8.4 %all-to-all-start = ((bf16[16,2,32768]{2,1,0:T(2,128)(2,1)}), bf16[16,2,32768]{2,1,0:T(2,128)(2,1)S(1)}, u32[]{:S(2)}, u32[]{:S(2)}) async-start(bf16[16,2,32768]{2,1,0:T(2,128)(2,1)} %reshape.243), calls=%async_computation | async-start | bytes 4194304 | tf_op jit(solution)/shard_map/all_to_all | solution.py:137
  41.2 0.0 all-reduce.4.cloned.1.call-start
  41.2 0.1 dynamic-slice_compare_fusion
  41.4 30.8 %all-to-all-done = bf16[16,2,32768]{2,1,0:T(2,128)(2,1)S(1)} async-done(((bf16[16,2,32768]{2,1,0:T(2,128)(2,1)}), bf16[16,2,32768]{2,1,0:T(2,128)(2,1)S(1)}, u32[]{:S(2)}, u32[]{:S(2)}) %all-to-all-start) | async-done | bytes 2097184 | tf_op jit(solution)/shard_map/all_to_all | solution.py:137
  72.1 5.0 %reshape.244 = bf16[256,4,16,64]{3,2,1,0:T(8,128)(2,1)} reshape(bf16[16,2,32768]{2,1,0:T(2,128)(2,1)S(1)} %all-to-all-done) | data formatting | bytes 4194304
  77.1 6.9 %copy.30 = bf16[16,64,4,16,16]{1,0,4,2,3:T(8,128)(2,1)} copy(bf16[16,64,4,16,16]{1,3,2,4,0:T(8,128)(2,1)} %bitcast.99) | data formatting | bytes 4194304 | tf_op jit(solution)/shard_map/all_to_all | solution.py:137
  84.0 5.5 %all_to_all.16 = bf16[1024,4,16,16]{0,3,1,2:T(8,128)(2,1)S(1)} reshape(bf16[16,64,4,16,16]{1,0,4,2,3:T(8,128)(2,1)} %copy.30) | data formatting | bytes 4194304 | tf_op jit(solution)/shard_map/all_to_all | solution.py:137
  89.5 1.1 fusion.46
  90.6 0.0 copy-start.10
  90.6 2.3 copy.31
  92.8 2.6 collective-permute-start
  95.4 2.2 copy.32
  97.7 1.5 collective-permute-start.1
  99.2 0.1 fusion.25
  99.4 0.2 fusion.23
  99.6 0.1 broadcast_or_fusion.1
  99.7 0.1 compare_and_fusion
  99.7 0.1 fusion.24
  99.9 4.6 %copy.36 = bf16[16,64,4,16,16]{1,0,4,3,2:T(8,128)(2,1)} copy(bf16[16,64,4,16,16]{1,3,2,4,0:T(8,128)(2,1)S(1)} %bitcast.100) | data formatting | bytes 4194304 | tf_op jit(solution)/shard_map/all_to_all | solution.py:137
  104.5 2.4 fusion.45
  106.9 4.9 %collective-permute-start.2 = (bf16[1024,4,14,16]{0,3,1,2:T(8,128)(2,1)}, bf16[1024,4,14,16]{0,3,1,2:T(8,128)(2,1)}, u32[]{:S(2)}, u32[]{:S(2)}) collective-permute-start(bf16[1024,4,14,16]{0,3,1,2:T(8,128)(2,1)} %get-tuple-element.6), channel_id=1, source_target_pairs={{0,1},{1,2},{2,3},{3,4},{4,5},{5,6},{6,7},{8,9},{9,10},{10,11},{11... | collective-permute-start | bytes 5505032 | tf_op jit(solution)/shard_map/ppermute | solution.py:21
  111.8 1.9 collective-permute-start.3
  113.7 6.5 %reshape.223 = bf16[1024,1024]{0,1:T(8,128)(2,1)} reshape(bf16[16,64,4,16,16]{1,0,4,3,2:T(8,128)(2,1)} %copy.36) | data formatting | bytes 4194304 | tf_op jit(solution)/shard_map/reshape | solution.py:159
  120.2 4.7 %convolution_bitcast_fusion.1 = f32[128,8,8,128]{3,2,1,0:T(8,128)S(1)} fusion(bf16[1024,1024]{0,1:T(8,128)(2,1)} %reshape.223), kind=kOutput, calls=%fused_computation.29 | convolution fusion | flops 2147483648 | bytes 6291456 | tf_op jit(solution)/shard_map/ik,jk->ij/dot_general | solution.py:161
  124.9 1.0 copy.57
  125.9 6.4 %collective-permute-done = bf16[1024,4,16,14]{0,2,3,1:T(8,128)(2,1)} collective-permute-done((bf16[1024,4,16,14]{0,2,3,1:T(8,128)(2,1)}, bf16[1024,4,16,14]{0,2,3,1:T(8,128)(2,1)}, u32[]{:S(2)}, u32[]{:S(2)}) %collective-permute-start) | collective-permute-done | bytes 1835040 | tf_op jit(solution)/shard_map/ppermute | solution.py:21
  132.3 2.5 copy.33
  134.8 4.9 %collective-permute-done.1 = bf16[1024,4,16,14]{0,2,3,1:T(8,128)(2,1)} collective-permute-done((bf16[1024,4,16,14]{0,2,3,1:T(8,128)(2,1)}, bf16[1024,4,16,14]{0,2,3,1:T(8,128)(2,1)}, u32[]{:S(2)}, u32[]{:S(2)}) %collective-permute-start.1) | collective-permute-done | bytes 1835040 | tf_op jit(solution)/shard_map/ppermute | solution.py:22
  139.7 2.5 copy.34
  142.2 0.0 copy-start.8
  142.2 2.0 fusion.26
  144.2 0.0 copy-done.8
  144.2 0.1 multiply_subtract_fusion
  144.3 0.1 multiply_convert_fusion
  144.4 0.1 fusion.47
  144.6 2.2 collective-permute-start.4
  146.8 1.3 collective-permute-start.5
  148.1 2.2 fusion.4
  150.4 0.0 collective-permute-done.2
  150.4 0.0 collective-permute-done.3
  150.4 11.6 %fusion.7 = bf16[1024,4,44,16]{0,3,1,2:T(8,128)(2,1)S(1)} fusion(bf16[1024,4,14,16]{0,3,1,2:T(8,128)(2,1)} %collective-permute-done.3, bf16[1024,4,14,16]{0,3,1,2:T(8,128)(2,1)} %collective-permute-done.2, bf16[1024,4,16,14]{0,3,1,2:T(8,128)(2,1)S(1)} %copy.34, bf16[1024,4,16,16]{0,3,1,2:T(8,128)(2,1)S(1)} %all_to_all.16, bf16[1024,4,16,14]{0,3,1,2:T(8,128)(2,1)S(1)} %copy.33), kind=kLoop, calls=%fused_computation.12 | loop fusion | flops 40370176 | bytes 15204352 | tf_op jit(solution)/shard_map/concatenate | solution.py:28
  162.0 6.6 %fusion.14 = f32[4,16,1024,16]{2,1,3,0:T(8,128)S(1)} fusion(bf16[1024,4,44,16]{0,3,1,2:T(8,128)(2,1)S(1)} %fusion.7, bf16[4,44,4,16,1]{1,0,2,3,4:T(4,128)(2,1)S(1)} %fusion.23), kind=kOutput, calls=%fused_computation.27 | convolution fusion | flops 369098752 | bytes 9984000 | tf_op jit(solution)/shard_map/odjz,djei->oeiz/dot_general | solution.py:94
  168.7 0.0 collective-permute-done.4
  168.7 3.2 fusion.12
  171.9 2.4 convolution_bitcast_fusion
  174.3 1.0 copy.58
  175.3 7.0 %pad_maximum_fusion = f32[2097152]{0:T(1024)} fusion(f32[1048576]{0:T(1024)S(1)} %bitcast.102, f32[1048576]{0:T(1024)S(1)} %bitcast.101), kind=kLoop, calls=%fused_computation.4 | loop fusion | flops 2097152 | bytes 16777216 | tf_op jit(solution)/shard_map/concatenate | solution.py:51
  182.4 0.0 all-reduce.4.cloned.1.call-update
  182.4 168.1 %all-reduce.4.cloned.1.call-done = f32[2097152]{0:T(1024)} async-done(((f32[2097152]{0:T(1024)}), f32[2097152]{0:T(1024)}) %all-reduce.4.cloned.1.call-update) | async-done | bytes 8388624 | tf_op jit(solution)/shard_map/psum | solution.py:52
  350.5 5.2 %fusion.10 = (bf16[1048576]{0:T(1024)(128)(2,1)}, bf16[1048576]{0:T(1024)(128)(2,1)S(1)}) fusion(f32[2097152]{0:T(1024)} %all-reduce.4.cloned.1.call-done), kind=kLoop, calls=%fused_computation.19 | loop fusion | flops 4194304 | bytes 12582912 | tf_op jit(solution)/shard_map/convert_element_type | solution.py:171
  355.7 4.2 %convert_element_type.74 = bf16[1024,1024]{1,0:T(8,128)(2,1)} reshape(bf16[1048576]{0:T(1024)(128)(2,1)} %get-tuple-element.4) | data formatting | bytes 4194304 | tf_op jit(solution)/shard_map/convert_element_type | solution.py:171
  359.9 6.5 %fusion.49 = f32[1024,1024]{0,1:T(8,128)} fusion(bf16[1024,1024]{1,0:T(8,128)(2,1)} %convert_element_type.74, bf16[1024,1024]{0,1:T(8,128)(2,1)} %reshape.223), kind=kOutput, calls=%fused_computation.82 | convolution fusion | flops 2147483648 | bytes 8388608 | tf_op jit(solution)/shard_map/dot_general | solution.py:172
  366.5 2.3 convert_element_type.78
  368.8 10.8 %subtract_convert_fusion = bf16[1024,1024]{0,1:T(8,128)(2,1)} fusion(bf16[1024,1024]{1,0:T(8,128)(2,1)} %convert_element_type.78, f32[1024,1024]{0,1:T(8,128)} %fusion.49, bf16[1024,1024]{0,1:T(8,128)(2,1)} %bitcast.104, bf16[1024,1024]{0,1:T(8,128)(2,1)} %reshape.223), kind=kOutput, calls=%fused_computation.24 | convolution fusion | flops 2165309440 | bytes 12582912 | tf_op jit(solution)/shard_map/dot_general | solution.py:176
  (27 shorter events, 0.1 us)
Async XLA Ops:
  7.2 92.2 %copy-start = (bf16[29,4,4]{0,2,1:T(4,128)(2,1)S(1)}, bf16[29,4,4]{0,2,1:T(4,128)(2,1)}, u32[]{:S(2)}) copy-start(bf16[29,4,4]{0,2,1:T(4,128)(2,1)} %param.13) | copy-start | bytes 2788
  7.2 10.1 %copy-start.7 = (s32[1024]{0:T(1024)S(1)}, s32[1024]{0:T(1024)}, u32[]{:S(2)}) copy-start(s32[1024]{0:T(1024)} %param.10) | copy-start | bytes 12292
  7.2 10.1 %copy-start.5 = (s32[1024]{0:T(1024)S(1)}, s32[1024]{0:T(1024)}, u32[]{:S(2)}) copy-start(s32[1024]{0:T(1024)} %param.9) | copy-start | bytes 12292
  25.2 16.0 %copy-start.9 = (s32[1024]{0:T(1024)S(1)}, s32[1024]{0:T(1024)}, u32[]{:S(2)}) copy-start(s32[1024]{0:T(1024)} %param.12) | copy-start | bytes 12292
  32.7 39.4 %all-to-all-start = ((bf16[16,2,32768]{2,1,0:T(2,128)(2,1)}), bf16[16,2,32768]{2,1,0:T(2,128)(2,1)S(1)}, u32[]{:S(2)}, u32[]{:S(2)}) async-start(bf16[16,2,32768]{2,1,0:T(2,128)(2,1)} %reshape.243), calls=%async_computation | async-start | bytes 4194304 | tf_op jit(solution)/shard_map/all_to_all | solution.py:137
  41.2 309.4 %all-reduce.4.cloned.1.call-start = ((), (), s32[]{:S(2)}) async-start(), calls=%async_computation.1 | async-start | bytes 16777216 | tf_op jit(solution)/shard_map/psum | solution.py:52
  90.6 8.7 %copy-start.10 = (bf16[16,4]{0,1:T(4,128)(2,1)S(1)}, bf16[16,4]{0,1:T(4,128)(2,1)}, u32[]{:S(2)}) copy-start(bf16[16,4]{0,1:T(4,128)(2,1)} %param.14) | copy-start | bytes 388
  90.6 9.3 %copy-start.2 = (bf16[256,4,16,64]{3,2,1,0:T(8,128)(2,1)S(1)}, bf16[256,4,16,64]{3,2,1,0:T(8,128)(2,1)}, u32[]{:S(2)}) copy-start(bf16[256,4,16,64]{3,2,1,0:T(8,128)(2,1)} %reshape.244) | copy-start | bytes 6291460
  92.8 39.5 %collective-permute-start = (bf16[1024,4,16,14]{0,2,3,1:T(8,128)(2,1)}, bf16[1024,4,16,14]{0,2,3,1:T(8,128)(2,1)}, u32[]{:S(2)}, u32[]{:S(2)}) collective-permute-start(bf16[1024,4,16,14]{0,2,3,1:T(8,128)(2,1)} %copy.31), channel_id=1, source_target_pairs={{0,8},{8,16},{16,24},{24,32},{32,40},{40,48},{48,56},{56,64},{64,7... | collective-permute-start | bytes 5505032 | tf_op jit(solution)/shard_map/ppermute | solution.py:21
  97.7 42.0 %collective-permute-start.1 = (bf16[1024,4,16,14]{0,2,3,1:T(8,128)(2,1)}, bf16[1024,4,16,14]{0,2,3,1:T(8,128)(2,1)}, u32[]{:S(2)}, u32[]{:S(2)}) collective-permute-start(bf16[1024,4,16,14]{0,2,3,1:T(8,128)(2,1)} %copy.32), channel_id=1, source_target_pairs={{8,0},{16,8},{24,16},{32,24},{40,32},{48,40},{56,48},{64,56},{72,6... | collective-permute-start | bytes 5505032 | tf_op jit(solution)/shard_map/ppermute | solution.py:22
  106.9 43.4 %collective-permute-start.2 = (bf16[1024,4,14,16]{0,3,1,2:T(8,128)(2,1)}, bf16[1024,4,14,16]{0,3,1,2:T(8,128)(2,1)}, u32[]{:S(2)}, u32[]{:S(2)}) collective-permute-start(bf16[1024,4,14,16]{0,3,1,2:T(8,128)(2,1)} %get-tuple-element.6), channel_id=1, source_target_pairs={{0,1},{1,2},{2,3},{3,4},{4,5},{5,6},{6,7},{8,9},{9,10},{10,11},{11... | collective-permute-start | bytes 5505032 | tf_op jit(solution)/shard_map/ppermute | solution.py:21
  111.8 38.6 %collective-permute-start.3 = (bf16[1024,4,14,16]{0,3,1,2:T(8,128)(2,1)}, bf16[1024,4,14,16]{0,3,1,2:T(8,128)(2,1)}, u32[]{:S(2)}, u32[]{:S(2)}) collective-permute-start(bf16[1024,4,14,16]{0,3,1,2:T(8,128)(2,1)} %get-tuple-element.7), channel_id=1, source_target_pairs={{1,0},{2,1},{3,2},{4,3},{5,4},{6,5},{7,6},{9,8},{10,9},{11,10},{12... | collective-permute-start | bytes 5505032 | tf_op jit(solution)/shard_map/ppermute | solution.py:22
  142.2 2.0 copy-start.8
  144.2 6.1 %copy-start.6 = (f32[16,16]{1,0:T(8,128)}, f32[16,16]{1,0:T(8,128)S(1)}, u32[]{:S(2)}) copy-start(f32[16,16]{1,0:T(8,128)S(1)} %get-tuple-element.12) | copy-start | bytes 3076
  144.6 24.1 %collective-permute-start.4 = (bf16[1024,16,14]{0,2,1:T(8,128)(2,1)S(1)}, bf16[1024,16,14]{0,2,1:T(8,128)(2,1)S(1)}, u32[]{:S(2)}, u32[]{:S(2)}) collective-permute-start(bf16[1024,16,14]{0,2,1:T(8,128)(2,1)S(1)} %get-tuple-element.10), channel_id=1, source_target_pairs={{0,8},{8,16},{16,24},{24,32},{32,40},{40,48},{48,56},{56,64},{64,7... | collective-permute-start | bytes 1376264 | tf_op jit(solution)/shard_map/ppermute | solution.py:41
  146.8 21.8 %collective-permute-start.5 = (bf16[1024,16,14]{0,2,1:T(8,128)(2,1)S(1)}, bf16[1024,16,14]{0,2,1:T(8,128)(2,1)S(1)}, u32[]{:S(2)}, u32[]{:S(2)}) collective-permute-start(bf16[1024,16,14]{0,2,1:T(8,128)(2,1)S(1)} %get-tuple-element.11), channel_id=1, source_target_pairs={{8,0},{16,8},{24,16},{32,24},{40,32},{48,40},{56,48},{64,56},{72,6... | collective-permute-start | bytes 1376264 | tf_op jit(solution)/shard_map/ppermute | solution.py:43
  168.6 3.2 copy-start.3
  171.8 2.5 copy-start.4
  368.8 10.8 %copy-start.1 = (bf16[29,4,4]{0,2,1:T(4,128)(2,1)S(1)}, bf16[29,4,4]{0,2,1:T(4,128)(2,1)}, u32[]{:S(2)}) copy-start(bf16[29,4,4]{0,2,1:T(4,128)(2,1)} %param.13) | copy-start | bytes 2788
Sparse Core Ops, SparseCore 0:
  182.5 167.9 all-reduce.3
where the time goes:
time: 391 us; the launch traced here: 387 us
  waiting for transfers between devices  210 us (54%)
  local copies, waits for them, and re-layouts  67.6 us (17%)
  matrix products  38.9 us (10%)
  other arithmetic  32.5 us (8%)
  starting transfers between devices  22.9 us (6%)
  between operations  14.6 us (4%)
    psum x1, waiting for transfers between devices, packed_total(): subtotal = lax.psum(line, axis)  168 us
    all_to_all x1, waiting for transfers between devices, local(): lax.all_to_all(masked, 'orb', split_axis=3, concat_axis=0, tiled=True)  30.8 us
    unnamed x27, local copies, waits for them, and re-layouts  23.4 us
    all_to_all x3, local copies, waits for them, and re-layouts, local(): lax.all_to_all(masked, 'orb', split_axis=3, concat_axis=0, tiled=True)  17 us
    concatenate x1, other arithmetic, padded(): jnp.concatenate([jnp.pad(low, around), x, jnp.pad(high, around)], axis=dim)  11.6 us
    dot_general x1, matrix products, local(): jnp.dot(intersection_round, trial, preferred_element_type=jnp.float32)  10.8 us
    all_to_all x1, starting transfers between devices, local(): lax.all_to_all(masked, 'orb', split_axis=3, concat_axis=0, tiled=True)  8.42 us
  transfers between devices with their start and end apart: 8, of which 4 were waited for; matrix products, arithmetic and copies ran while one was open for 13% of the time, Pallas kernels for 0%

commit v1 on v0

v1 whole, which is shorter than its diff:
```python
import functools

import jax
import jax.numpy as jnp
from jax import lax
from jax.experimental import pallas as pl
from jax.experimental.pallas import tpu as pltpu
from jax.sharding import PartitionSpec as P

ZB = 16
xc_factor = 0.98474502
step_length = 0.1
f32, bf16 = jnp.float32, jnp.bfloat16

MESH = pl.DeviceIdType.MESH


def coords():
    orb, comp = lax.axis_index("orb"), lax.axis_index("comp")
    return orb // 4, orb % 4, comp // 2, comp % 2


def at(z, x, y, core):
    return {"orb": z * 4 + x, "comp": y * 2 + core}


def turned(pos, axis, step):
    pos = list(pos)
    pos[axis] = lax.rem(pos[axis] + step, 4)
    return tuple(pos)


def greet(targets):
    barrier = pltpu.get_barrier_semaphore()
    for t in targets:
        pl.semaphore_signal(barrier, inc=1, device_id=t, device_id_type=MESH)
    pl.semaphore_wait(barrier, len(targets))


def rows_at(i, size):
    return pl.ds(pl.multiple_of(i * size, size), size)


def eye(n):
    return (
        lax.broadcasted_iota(jnp.int32, (n, n), 0) == lax.broadcasted_iota(jnp.int32, (n, n), 1)
    ).astype(bf16)


def band(row):
    wide = jnp.broadcast_to(row, (256, 256))
    rolled = pltpu.roll(wide, 0, 1, stride=1, stride_axis=0)
    gap = lax.broadcasted_iota(jnp.int32, (256, 256), 0) - lax.broadcasted_iota(jnp.int32, (256, 256), 1)
    return jnp.where((gap <= 14) & (gap >= -14), rolled, 0.0).astype(bf16)


def inside_planes(start_ref, len_ref, first_orbital, first_plane, o):
    begin = start_ref[first_orbital + o] - first_plane
    plane = lax.broadcasted_iota(jnp.int32, (16, 256), 0)
    return (plane >= begin) & (plane < begin + len_ref[first_orbital + o])


def fine_points(fine_ref):
    spread = (
        lax.broadcasted_iota(jnp.int32, (16, 256), 1) // ZB == lax.broadcasted_iota(jnp.int32, (16, 256), 0)
    ).astype(bf16)
    return jnp.dot((fine_ref[...] > 0).astype(f32).astype(bf16), spread, preferred_element_type=f32)


def pack(wide_lo, wide_hi, pack_ref):
    unit = eye(256)

    def step(j, _):
        halves = []
        for ref in (wide_lo, wide_hi):
            halves.append(
                jnp.concatenate([ref[pl.ds(j, 64, stride=64), :], ref[pl.ds(j + 32, 64, stride=64), :]], axis=0)
            )
        both = jnp.concatenate(halves, axis=1).astype(bf16)
        turned_over = lax.dot_general(unit, both, (((1,), (1,)), ((), ())), preferred_element_type=f32).astype(bf16)
        for q in range(16):
            pack_ref[q, rows_at(j, 16), :] = turned_over[q * 16 : q * 16 + 16, :]
        return 0

    lax.fori_loop(0, 32, step, 0, unroll=4)


def first_kernel(start_ref, len_ref, occ_ref, psi_ref, fine_ref, base_ref, masked_ref, pack_ref, values_ref, part_ref, lo, hi):
    first_orbital = lax.axis_index("orb") * 64
    first_plane = lax.axis_index("comp") * 16
    fine = fine_points(fine_ref) > 0.5

    def mask(o, _):
        inside = inside_planes(start_ref, len_ref, first_orbital, first_plane, o)
        for c in range(4):
            on = inside if c == 0 else inside & fine
            value = jnp.where(on, psi_ref[o, c].astype(f32), 0.0)
            masked_ref[o, c] = value.astype(bf16)
            rows = pl.ds(pl.multiple_of(o * 64 + c * 16, 16), 16)
            lo[rows, :] = value[:, :128]
            hi[rows, :] = value[:, 128:]
        return 0

    lax.fori_loop(0, 64, mask, 0, unroll=2)
    forward = [band(base_ref[pl.ds(16 + d, 1), :]) for d in range(4)]

    def block(i, total):
        got = jnp.zeros((256, 256), f32)
        for d in range(4):
            rows = masked_ref[rows_at(i, 16), d].reshape(256, 256)
            got = got + jnp.dot(rows, forward[d], preferred_element_type=f32)
        for n in range(16):
            one = got[n * 16 : n * 16 + 16]
            values_ref[i * 16 + n] = one
            total = total + occ_ref[first_orbital + i * 16 + n].astype(f32) * (one * one)
        return total

    part_ref[...] = lax.fori_loop(0, 4, block, jnp.zeros((16, 256), f32))
    pack(lo, hi, pack_ref)


VM = pl.BlockSpec(memory_space=pltpu.VMEM)
SM = pl.BlockSpec(memory_space=pltpu.SMEM)
HB = pl.BlockSpec(memory_space=pl.ANY)


def shape(dims, kind=bf16):
    return jax.ShapeDtypeStruct(dims, kind)


def first_step(start, length, occupation, psi, fine, base):
    return pl.pallas_call(
        first_kernel,
        out_shape=(shape((64, 4, 16, 256)), shape((16, 512, 128)), shape((64, 16, 256), f32), shape((16, 256), f32)),
        in_specs=[SM, SM, SM, VM, VM, VM],
        out_specs=(VM, VM, VM, VM),
        scratch_shapes=[pltpu.VMEM((4096, 128), f32)] * 2,
        compiler_params=pltpu.CompilerParams(vmem_limit_bytes=40 << 20),
        name="first",
    )(start, length, occupation, psi, fine, base)


def plane_steps():
    return [(s, t) for s in range(4) for t in range(4) if s or t]


GROUPS = ((0, 1024, 2, (0, 1)), (1024, 512, 1, (0, 2)), (1536, 512, 0, (1, 2)))


def remote(src, dst, ssem, rsem, to):
    return pltpu.make_async_remote_copy(
        src_ref=src, dst_ref=dst, send_sem=ssem, recv_sem=rsem, device_id=to, device_id_type=MESH
    )


class Group:
    def __init__(self, g, scale, w_ref, out_ref, h_in, h_sum, q_in, q_sum, f_in, f_sum, sems):
        self.g, self.scale = g, scale
        self.w, self.out, self.h_in, self.h_sum = w_ref, out_ref, h_in, h_sum
        self.q_in, self.q_sum, self.f_in, self.f_sum = q_in, q_sum, f_in, f_sum
        self.sems = sems
        self.col, self.width, self.axis, self.plane = GROUPS[g]
        self.cols = pl.ds(self.col, self.width)
        self.here = coords()
        z, x, y, core = self.here
        self.mate = at(z, x, y, 1 - core)
        self.keep = pl.multiple_of(core * 512, 512)
        self.give = pl.multiple_of(512 - core * 512, 512)
        self.sent = []

    def begin(self):
        s0, r0 = self.sems[0:2]
        rows = pl.ds(self.give, 512)
        self.copy0 = remote(self.w.at[rows, self.cols], self.h_in.at[:, self.cols], s0.at[self.g], r0.at[self.g], self.mate)
        self.copy0.start()

    def to_axis(self):
        s1, r1 = self.sems[2:4]
        self.copy0.wait()

        def add(i, _):
            rows = rows_at(i, 32)
            mine = pl.ds(pl.multiple_of(self.keep + i * 32, 32), 32)
            total = self.w[mine, self.cols].astype(f32) + self.h_in[rows, self.cols].astype(f32)
            self.h_sum[rows, self.cols] = total.astype(bf16)
            return 0

        lax.fori_loop(0, 16, add, 0)
        self.copies1 = []
        for s in (2, 1, 3):
            to = turned(self.here, self.axis, s)
            rows = pl.ds(pl.multiple_of(to[self.axis] * 128, 128), 128)
            c = remote(self.h_sum.at[rows, self.cols], self.q_in.at[s - 1], s1.at[self.g, s - 1], r1.at[self.g, s - 1], at(*to))
            c.start()
            self.copies1.append(c)
        self.sent += self.copies1

    def piece(self, pos):
        b = pos[self.plane[0]] * 4 + pos[self.plane[1]]
        half = self.width // 2
        return (b // 2) * 16, (b % 2) * half, half

    def to_plane(self):
        s2, r2 = self.sems[4:6]
        for c in self.copies1:
            c.wait_recv()
        base = pl.multiple_of(self.here[self.axis] * 128, 128)

        def add(i, _):
            rows = rows_at(i, 16)
            total = self.h_sum[pl.ds(pl.multiple_of(base + i * 16, 16), 16), self.cols].astype(f32)
            for s in range(3):
                total = total + self.q_in[s, rows, :].astype(f32)
            self.q_sum[rows, :] = total.astype(bf16)
            return 0

        lax.fori_loop(0, 8, add, 0)
        self.copies2 = []
        for n, (s, t) in enumerate(plane_steps()):
            to = turned(turned(self.here, self.plane[0], s), self.plane[1], t)
            row, col, half = self.piece(to)
            src = self.q_sum.at[pl.ds(pl.multiple_of(row, 16), 16), pl.ds(pl.multiple_of(col, 128), half)]
            c = remote(src, self.f_in.at[n], s2.at[self.g, n], r2.at[self.g, n], at(*to))
            c.start()
            self.copies2.append(c)
        self.sent += self.copies2

    def from_plane(self):
        t2, u2 = self.sems[6:8]
        for c in self.copies2:
            c.wait_recv()
        row, col, half = self.piece(self.here)
        total = self.q_sum[pl.ds(pl.multiple_of(row, 16), 16), pl.ds(pl.multiple_of(col, 128), half)].astype(f32)
        for n in range(15):
            total = total + self.f_in[n].astype(f32)
        self.f_sum[...] = (total * self.scale).astype(bf16)
        spot = self.out.at[
            pl.ds(pl.multiple_of(self.keep + self.here[self.axis] * 128 + row, 16), 16),
            pl.ds(pl.multiple_of(self.col + col, 128), half),
        ]
        self.copies3 = []
        for n, (s, t) in enumerate(plane_steps()):
            to = turned(turned(self.here, self.plane[0], s), self.plane[1], t)
            c = remote(self.f_sum, spot, t2.at[self.g, n], u2.at[self.g, n], at(*to))
            c.start()
            self.copies3.append(c)
        self.own = pltpu.make_async_copy(self.f_sum, spot, t2.at[self.g, 15])
        self.own.start()
        self.sent += self.copies3

    def from_axis(self):
        t1, u1 = self.sems[8:10]
        self.own.wait()
        for c in self.copies3:
            c.wait_recv()
        spot = self.out.at[pl.ds(pl.multiple_of(self.keep + self.here[self.axis] * 128, 128), 128), self.cols]
        self.copies4 = []
        for s in (2, 1, 3):
            c = remote(spot, spot, t1.at[self.g, s - 1], u1.at[self.g, s - 1], at(*turned(self.here, self.axis, s)))
            c.start()
            self.copies4.append(c)
        self.sent += self.copies4

    def to_mate(self):
        t0, u0 = self.sems[10:12]
        for c in self.copies4:
            c.wait_recv()
        spot = self.out.at[pl.ds(self.keep, 512), self.cols]
        self.copy5 = remote(spot, spot, t0.at[self.g], u0.at[self.g], self.mate)
        self.copy5.start()

    def finish(self):
        self.copy5.wait()
        for c in self.sent:
            c.wait_send()


def spread_copies(pack_ref, got_ref, send, recv):
    here = coords()
    me = here[0] * 4 + here[1]
    copies = []
    for n, (s, t) in enumerate(plane_steps()):
        to = turned(turned(here, 0, s), 1, t)
        copies.append(remote(pack_ref.at[to[0] * 4 + to[1]], got_ref.at[me], send.at[n], recv.at[n], at(*to)))
    return copies, pltpu.make_async_copy(pack_ref.at[me], got_ref.at[me], send.at[15])


def mover():
    l = lax.broadcasted_iota(jnp.int32, (256, 256), 0)
    n = lax.broadcasted_iota(jnp.int32, (256, 256), 1)
    swapped = jnp.where((n >= 64) & (n < 128), n + 64, jnp.where((n >= 128) & (n < 192), n - 64, n))
    return (l == swapped).astype(bf16)


def main_kernel(
    scale, start_ref, len_ref, masked_ref, pack_ref, values_ref, part_ref, ext_ref, fine_ref, base_ref,
    density_ref, xt_ref, at_ref, out_ref,
    got, low, high, parts, lo, hi, weighted, bands, across, pack_a, got_a, x_rows, w, h_in, h_sum, *rest,
):
    q_in, q_sum, f_in, f_sum = rest[0:3], rest[3:6], rest[6:9], rest[9:12]
    sems = rest[12:24]
    sd, rd, sh, rh, sx, rx, sa, ra = rest[24:]
    here = coords()
    z, x, y, core = here
    orb, comp = lax.axis_index("orb"), lax.axis_index("comp")
    first_orbital, first_plane = orb * 64, comp * 16
    targets = [at(z, x, y, 1 - core), at(z, x, lax.rem(y + 3 + 2 * core, 4), 1 - core)]
    for a in (0, 1, 2):
        targets += [at(*turned(here, a, s)) for s in (1, 2, 3)]
    for a, b in ((0, 1), (0, 2), (1, 2)):
        targets += [at(*turned(turned(here, a, s), b, t)) for s in (1, 2, 3) for t in (1, 2, 3)]
    greet(targets)

    density_copies = []
    for n, (s, t) in enumerate(plane_steps()):
        to = turned(turned(here, 0, s), 1, t)
        density_copies.append(remote(part_ref, parts.at[n], sd.at[n], rd.at[n], at(*to)))
    halo_copies = [
        remote(masked_ref, low, sh.at[0], rh.at[0], {"orb": orb, "comp": lax.rem(comp + 1, 8)}),
        remote(masked_ref, high, sh.at[1], rh.at[1], {"orb": orb, "comp": lax.rem(comp + 7, 8)}),
    ]
    spread_x, own_x = spread_copies(pack_ref, got, sx, rx)
    spread_a, own_a = spread_copies(pack_a, got_a, sa, ra)
    for c in density_copies + halo_copies + spread_x + [own_x]:
        c.start()

    fine = fine_points(fine_ref) > 0.5

    def build(n, _):
        bands[n] = band(base_ref[pl.ds(n, 1), :])
        return 0

    lax.fori_loop(0, 16, build, 0, unroll=2)
    for e in range(4):
        bands[16 + e] = band(base_ref[pl.ds(20 + e, 1), :])
    spot = lax.rem(lax.broadcasted_iota(jnp.int32, (16, 256), 1), 48)
    edge = ((comp == 0) & (spot < 16)) | ((comp == 7) & (spot >= 32))
    for e in range(4):
        rolled = pltpu.roll(jnp.broadcast_to(base_ref[pl.ds(24 + e, 1), :], (16, 256)), 0, 1, stride=1, stride_axis=0)
        across[pl.ds(e * 16, 16), :] = jnp.where(edge, 0.0, rolled).astype(bf16)

    density = part_ref[...]
    for n in range(15):
        density_copies[n].wait_recv()
        density = density + parts[n]
    density_ref[...] = density
    potential = ext_ref[...] - xc_factor * jnp.exp(jnp.log(density) * (1.0 / 3.0))

    def weigh(o, _):
        weighted[o] = (potential * values_ref[o]).astype(bf16)
        return 0

    lax.fori_loop(0, 64, weigh, 0, unroll=4)

    def along(i, _):
        for e in range(4):
            total = jnp.dot(weighted[rows_at(i, 16)].reshape(256, 256), bands[16 + e], preferred_element_type=f32)
            for d in range(4):
                rows = masked_ref[rows_at(i, 16), d].reshape(256, 256)
                total = total + jnp.dot(rows, bands[d * 4 + e], preferred_element_type=f32)
            for n in range(16):
                rows = pl.ds(pl.multiple_of((i * 16 + n) * 64 + e * 16, 16), 16)
                lo[rows, :] = total[n * 16 : n * 16 + 16, :128]
                hi[rows, :] = total[n * 16 : n * 16 + 16, 128:]
        return 0

    lax.fori_loop(0, 4, along, 0)
    for c in halo_copies:
        c.wait_recv()

    def cross(o, _):
        window = jnp.concatenate([ref[o, d] for d in range(4) for ref in (low, masked_ref, high)], axis=0)
        summed = jnp.dot(across[:, :192], window, preferred_element_type=f32)
        inside = inside_planes(start_ref, len_ref, first_orbital, first_plane, o)
        for e in range(4):
            on = inside if e == 0 else inside & fine
            rows = pl.ds(pl.multiple_of(o * 64 + e * 16, 16), 16)
            part = summed[e * 16 : e * 16 + 16]
            lo[rows, :] = jnp.where(on[:, :128], part[:, :128] + lo[rows, :], 0.0)
            hi[rows, :] = jnp.where(on[:, 128:], part[:, 128:] + hi[rows, :], 0.0)
        return 0

    lax.fori_loop(0, 64, cross, 0, unroll=4)
    pack(lo, hi, pack_a)
    for c in spread_a + [own_a]:
        c.start()

    move = mover()
    own_x.wait()
    for c in spread_x:
        c.wait_recv()

    def unpack_x(m, _):
        pair = jnp.concatenate([got[2 * m], got[2 * m + 1]], axis=1)
        turned_back = jnp.dot(pair, move, preferred_element_type=f32).astype(bf16)
        lanes = pl.ds(pl.multiple_of(128 * m, 128), 128)
        xt_ref[0:512, lanes] = turned_back[:, :128]
        xt_ref[512:1024, lanes] = turned_back[:, 128:]
        rows = lax.dot_general(move, pair, (((1,), (1,)), ((), ())), preferred_element_type=f32).astype(bf16)
        x_rows[lanes, 0:512] = rows[:128]
        x_rows[lanes, 512:1024] = rows[128:]
        return 0

    lax.fori_loop(0, 8, unpack_x, 0)
    groups = [
        Group(g, scale, w, out_ref, h_in, h_sum, q_in[g], q_sum[g], f_in[g], f_sum[g], sems) for g in range(3)
    ]
    overlap, first, second = groups

    def overlaps(i, _):
        rows = rows_at(i, 128)
        w[rows, 0:1024] = jnp.dot(x_rows[rows, :], xt_ref[...], preferred_element_type=f32).astype(bf16)
        return 0

    lax.fori_loop(0, 8, overlaps, 0)
    overlap.begin()
    overlap.to_axis()
    overlap.to_plane()
    own_a.wait()
    for c in spread_a:
        c.wait_recv()

    def unpack_a(m, _):
        pair = jnp.concatenate([got_a[2 * m], got_a[2 * m + 1]], axis=1)
        turned_back = jnp.dot(pair, move, preferred_element_type=f32).astype(bf16)
        lanes = pl.ds(pl.multiple_of(128 * m, 128), 128)
        at_ref[0:512, lanes] = turned_back[:, :128]
        at_ref[512:1024, lanes] = turned_back[:, 128:]
        return 0

    lax.fori_loop(0, 8, unpack_a, 0)

    def multipliers(i, _):
        rows = rows_at(i, 128)
        w[rows, 1024:2048] = jnp.dot(x_rows[rows, :], at_ref[...], preferred_element_type=f32).astype(bf16)
        return 0

    lax.fori_loop(0, 8, multipliers, 0)
    first.begin()
    second.begin()
    overlap.from_plane()
    first.to_axis()
    second.to_axis()
    overlap.from_axis()
    first.to_plane()
    second.to_plane()
    first.from_plane()
    second.from_plane()
    first.from_axis()
    second.from_axis()
    overlap.to_mate()
    first.to_mate()
    second.to_mate()
    for c in density_copies + halo_copies + spread_x + spread_a:
        c.wait_send()
    for group in groups:
        group.finish()


def main_step(scale, start, length, masked, packed, values, part, external, fine, base):
    dma = pltpu.SemaphoreType.DMA
    vm = pltpu.VMEM
    widths = [g[1] for g in GROUPS]
    spread_buffer = vm((16, 512, 128), bf16)
    square = (1024, 1024)
    return pl.pallas_call(
        functools.partial(main_kernel, scale),
        out_shape=(shape((16, 256), f32), shape(square), shape(square), shape((1024, 2048))),
        in_specs=[SM, SM] + [VM] * 7,
        out_specs=(VM,) * 4,
        scratch_shapes=[spread_buffer, vm(masked.shape, bf16), vm(masked.shape, bf16), vm((15, 16, 256), f32)]
        + [vm((4096, 128), f32)] * 2
        + [vm((64, 16, 256), bf16), vm((20, 256, 256), bf16), vm((64, 256), bf16), spread_buffer, spread_buffer]
        + [vm(square, bf16), vm((1024, 2048), bf16), vm((512, 2048), bf16), vm((512, 2048), bf16)]
        + [vm((3, 128, n), bf16) for n in widths]
        + [vm((128, n), bf16) for n in widths]
        + [vm((15, 16, n // 2), bf16) for n in widths]
        + [vm((16, n // 2), bf16) for n in widths]
        + [dma((3,)), dma((3,)), dma((3, 3)), dma((3, 3)), dma((3, 15)), dma((3, 15))]
        + [dma((3, 16)), dma((3, 15)), dma((3, 3)), dma((3, 3)), dma((3,)), dma((3,))]
        + [dma((15,)), dma((15,)), dma((2,)), dma((2,)), dma((16,)), dma((15,)), dma((16,)), dma((15,))],
        compiler_params=pltpu.CompilerParams(collective_id=3, has_side_effects=True, vmem_limit_bytes=VMEM_MAIN),
        name="main",
    )(start, length, masked, packed, values, part, external, fine, base)


VMEM_MAIN = 52 << 20

def filter_rows(kinetic_taps, magic_taps):
    def ring(rows, before):
        rows = jnp.pad(rows, ((0, 0), (0, 256 - rows.shape[1])))
        return jnp.roll(rows, -before, axis=1)

    taps = jnp.transpose(kinetic_taps.astype(f32), (2, 1, 0))
    magic = jnp.transpose(magic_taps.astype(f32))
    across = jnp.pad(jnp.transpose(kinetic_taps.astype(f32), (1, 2, 0)), ((0, 0), (0, 0), (2, 17))).reshape(4, 192)
    return jnp.concatenate(
        [
            ring(taps.reshape(16, 29)[:, ::-1], 14),
            ring(magic[:, ::-1], 8),
            ring(magic, 7),
            jnp.pad(across, ((0, 0), (0, 64))),
        ],
        axis=0,
    )


def local(psi, region_start, region_len, fine_mask, occupation, kinetic_taps, magic_taps, external):
    base = filter_rows(kinetic_taps, magic_taps)
    masked, packed, values, part = first_step(region_start, region_len, occupation, psi, fine_mask, base)
    density, masked_k, applied_k, both = main_step(
        1.0 / 32768, region_start, region_len, masked, packed, values, part, external, fine_mask, base
    )
    density = lax.dynamic_slice_in_dim(density, lax.axis_index("orb") * 16, 16, 1)
    intersection_round, lagrange_round = both[:, :1024], both[:, 1024:]
    gradient = applied_k.astype(f32) - jnp.dot(masked_k, lagrange_round, preferred_element_type=f32)
    trial = (masked_k.astype(f32) - step_length * gradient).astype(bf16)
    following = 1.5 * trial.astype(f32) - 0.5 * jnp.dot(trial, intersection_round, preferred_element_type=f32)
    psi_next = jnp.transpose(following.astype(bf16).reshape(4, 16, 16, 1024), (3, 0, 1, 2))
    return (density, psi_next)


def solution(mesh):
    return jax.shard_map(
        local,
        mesh=mesh,
        in_specs=(
            P("orb", None, "comp", None),
            P(),
            P(),
            P("comp", None),
            P(),
            P(),
            P(),
            P("comp", None),
        ),
        out_specs=(P("comp", "orb"), P(None, None, "comp", "orb")),
        check_vma=False,
    )
```

time: 391 us -> 158 us (0.40)
  waiting for transfers between devices: 210 us -> 0 us
  Pallas kernels: 0 us -> 135 us
  local copies, waits for them, and re-layouts: 67.6 us -> 11.4 us
  other arithmetic: 32.5 us -> 1.46 us
  matrix products: 38.9 us -> 8.71 us
  starting transfers between devices: 22.9 us -> 0 us
  between operations: 14.6 us -> 0.7 us
    psum x1 -> x0, waiting for transfers between devices: 168 us -> none  [packed_total(): subtotal = lax.psum(line, axis)]
    pallas_call x0 -> x2, Pallas kernels: none -> 135 us  [the longest x1 128 us: main_step(): pl.pallas_call(functools.partial(main_kernel, scale), out_shape=(shape((1...]
    all_to_all x1 -> x0, waiting for transfers between devices: 30.8 us -> none  [local(): lax.all_to_all(masked, 'orb', split_axis=3, concat_axis=0, tiled=True)]
    dot_general x11 -> x2, matrix products: 38.9 us -> 8.71 us  [the longest x1 4.69 us: local(): jnp.dot(masked_k, lagrange_round, preferred_element_type=f32)]
    concatenate x2 -> x1, other arithmetic: 18.7 us -> 0.08 us  [filter_rows(): jnp.concatenate([ring(taps.reshape(16, 29)[:, ::-1], 14), ring(magic[:, :...]
    all_to_all x3 -> x0, local copies, waits for them, and re-layouts: 17 us -> none  [local(): lax.all_to_all(masked, 'orb', split_axis=3, concat_axis=0, tiled=True)]
    ppermute x6 -> x0, starting transfers between devices: 14.4 us -> none  [the longest x2 7.46 us: padded(): lax.ppermute(last, axis, up)]
    unnamed x27 -> x28, local copies, waits for them, and re-layouts: 23.4 us -> 9.82 us
  transfers between devices with their start and end apart: 8 -> 0, of which waited for: 4 -> 0; matrix products, arithmetic and copies ran while one was open for 13% -> 0% of each run, Pallas kernels for 0% -> 0%
where the time goes in v1:
time: 158 us; the launch traced here: 157 us
  Pallas kernels  135 us (85%)
  local copies, waits for them, and re-layouts  11.4 us (7%)
  matrix products  8.71 us (6%)
    pallas_call x1, Pallas kernels, main_step(): pl.pallas_call(functools.partial(main_kernel, scale), out_shape=(shape((1...  128 us
    unnamed x28, local copies, waits for them, and re-layouts  9.82 us
    pallas_call x1, Pallas kernels, first_step(): pl.pallas_call(first_kernel, out_shape=(shape((64, 4, 16, 256)), shape((1...  7.1 us
    dot_general x1, matrix products, local(): jnp.dot(masked_k, lagrange_round, preferred_element_type=f32)  4.69 us
    dot_general x1, matrix products, local(): jnp.dot(trial, intersection_round, preferred_element_type=f32)  4.01 us

profile of v1, /device:TPU:1, one launch (start us, length us, event | category | flops | bytes accessed | tf_op | source)
XLA Modules:
  0.0 157.3 jit_solution(4800378259974205470)
XLA Ops:
  0.6 0.7 convert_bitcast_fusion.2
  1.3 0.1 slice.43
  1.4 0.1 slice.44
  1.5 0.1 rev.7
  1.6 0.1 pad_slice_fusion.2
  1.7 0.1 pad_slice_fusion.1
  1.7 0.7 convert_bitcast_fusion.1
  2.4 0.1 slice.49
  2.5 0.1 rev.6
  2.6 0.1 slice.41
  2.6 0.1 pad_slice_fusion
  2.7 0.1 pad.22
  2.8 0.1 reshape.14
  2.9 0.1 select_maximum_fusion.base_ref
  3.0 0.0 copy-start
  3.0 1.6 %copy-done = bf16[64,4,16,256]{3,2,1,0:T(8,128)(2,1)S(1)} copy-done((bf16[64,4,16,256]{3,2,1,0:T(8,128)(2,1)S(1)}, bf16[64,4,16,256]{3,2,1,0:T(8,128)(2,1)}, u32[]{:S(2)}) %copy-start) | copy-done | bytes 2097176
  4.6 0.0 copy-start.3
  4.6 0.7 copy-done.3
  5.3 0.0 copy-start.6
  5.3 0.7 copy-done.6
  5.9 0.0 copy-start.8
  6.0 0.7 copy-done.8
  6.6 0.0 copy-start.10
  6.6 0.7 copy-done.10
  7.3 7.1 %first.1 = (bf16[64,4,16,256]{3,2,1,0:T(8,128)(2,1)S(1)}, bf16[16,512,128]{2,1,0:T(8,128)(2,1)S(1)}, f32[64,16,256]{2,1,0:T(8,128)S(1)}, f32[16,256]{1,0:T(8,128)S(1)}) custom-call(s32[1024]{0:T(1024)S(1)} %copy-done.6, s32[1024]{0:T(1024)S(1)} %copy-done.8, s32[1024]{0:T(1024)S(1)} %copy-done.10, bf16[64,4,16,256]{3,2,1,0:T(8,128)(2,1)S(1)} %copy-done, ...), custom_call_target="tpu_custom_call" | custom-call | tf_op jit(solution)/shard_map/first/pallas_call | solution.py:132
  14.4 0.0 copy-start.1
  14.4 1.3 copy-done.1
  15.8 0.0 copy-start.2
  15.8 1.4 copy-done.2
  17.1 0.0 copy-start.4
  17.1 0.7 copy-done.4
  17.8 0.0 copy-start.5
  17.8 0.7 copy-done.5
  18.5 0.0 copy-start.7
  18.5 0.7 copy-done.7
  19.2 0.0 copy-start.9
  19.2 0.7 copy-done.9
  19.9 127.9 %main.1 = (f32[16,256]{1,0:T(8,128)S(1)}, bf16[1024,1024]{1,0:T(8,128)(2,1)}, bf16[1024,1024]{1,0:T(8,128)(2,1)}, bf16[1024,2048]{1,0:T(8,128)(2,1)}) custom-call(s32[1024]{0:T(1024)S(1)} %copy-done.7, s32[1024]{0:T(1024)S(1)} %copy-done.9, bf16[64,4,16,256]{3,2,1,0:T(8,128)(2,1)} %copy-done.1, bf16[16,512,128]{2,1,0:T(8,128)(2,1)} %copy-done.2, ...), custom_call_target="tpu_custom_call" | custom-call | tf_op jit(solution)/shard_map/main/pallas_call | solution.py:466
  147.8 0.7 constant_dynamic-slice_fusion
  148.5 0.0 copy-start.11
  148.5 0.0 copy-start.12
  148.5 0.0 copy-start.13
  148.5 4.7 %fusion.2 = f32[1024,1024]{1,0:T(8,128)S(1)} fusion(bf16[1024,1024]{1,0:T(8,128)(2,1)} %get-tuple-element.15, bf16[1024,2048]{1,0:T(8,128)(2,1)} %get-tuple-element.17), kind=kOutput, calls=%fused_computation.4 | convolution fusion | flops 2147483648 | bytes 8388608 | tf_op jit(solution)/shard_map/dot_general | solution.py:516
  153.2 0.0 copy-done.11
  153.2 0.0 copy-done.12
  153.2 0.0 copy-done.13
  153.2 4.0 %subtract_convert_fusion = bf16[1024,1024]{1,0:T(8,128)(2,1)} fusion(f32[1024,1024]{1,0:T(8,128)S(1)} %fusion.2, bf16[1024,1024]{1,0:T(8,128)(2,1)S(1)} %copy-done.13, bf16[1024,1024]{1,0:T(8,128)(2,1)S(1)} %copy-done.12, bf16[1024,2048]{1,0:T(8,128)(2,1)S(1)} %copy-done.11), kind=kOutput, calls=%fused_computation | convolution fusion | flops 2165309440 | bytes 20971520 | tf_op jit(solution)/shard_map/dot_general | solution.py:518
  (1 shorter events, 0.0 us)
Async XLA Ops:
  3.0 1.6 %copy-start = (bf16[64,4,16,256]{3,2,1,0:T(8,128)(2,1)S(1)}, bf16[64,4,16,256]{3,2,1,0:T(8,128)(2,1)}, u32[]{:S(2)}) copy-start(bf16[64,4,16,256]{3,2,1,0:T(8,128)(2,1)} %psi_ref.1) | copy-start | bytes 6291460
  4.6 0.7 copy-start.3
  5.3 0.7 copy-start.6
  5.9 0.7 copy-start.8
  6.6 0.7 copy-start.10
  14.4 1.3 copy-start.1
  15.8 1.4 copy-start.2
  17.1 0.7 copy-start.4
  17.8 0.7 copy-start.5
  18.5 0.7 copy-start.7
  19.2 0.7 copy-start.9
  148.5 4.7 %copy-start.11 = (bf16[1024,2048]{1,0:T(8,128)(2,1)S(1)}, bf16[1024,2048]{1,0:T(8,128)(2,1)}, u32[]{:S(2)}) copy-start(bf16[1024,2048]{1,0:T(8,128)(2,1)} %get-tuple-element.17) | copy-start | bytes 12582916
  148.5 4.7 %copy-start.12 = (bf16[1024,1024]{1,0:T(8,128)(2,1)S(1)}, bf16[1024,1024]{1,0:T(8,128)(2,1)}, u32[]{:S(2)}) copy-start(bf16[1024,1024]{1,0:T(8,128)(2,1)} %get-tuple-element.15) | copy-start | bytes 6291460
  148.5 4.7 %copy-start.13 = (bf16[1024,1024]{1,0:T(8,128)(2,1)S(1)}, bf16[1024,1024]{1,0:T(8,128)(2,1)}, u32[]{:S(2)}) copy-start(bf16[1024,1024]{1,0:T(8,128)(2,1)} %get-tuple-element.16) | copy-start | bytes 6291460

commit v2 on v1

v2 whole, which is shorter than its diff:
```python
import functools

import jax
import jax.numpy as jnp
from jax import lax
from jax.experimental import pallas as pl
from jax.experimental.pallas import tpu as pltpu
from jax.sharding import PartitionSpec as P

ZB = 16
xc_factor = 0.98474502
step_length = 0.1
f32, bf16 = jnp.float32, jnp.bfloat16

MESH = pl.DeviceIdType.MESH


def coords():
    orb, comp = lax.axis_index("orb"), lax.axis_index("comp")
    return orb // 4, orb % 4, comp // 2, comp % 2


def at(z, x, y, core):
    return {"orb": z * 4 + x, "comp": y * 2 + core}


def turned(pos, axis, step):
    pos = list(pos)
    pos[axis] = lax.rem(pos[axis] + step, 4)
    return tuple(pos)


def rows_at(i, size):
    return pl.ds(pl.multiple_of(i * size, size), size)


def eye(n):
    return (
        lax.broadcasted_iota(jnp.int32, (n, n), 0) == lax.broadcasted_iota(jnp.int32, (n, n), 1)
    ).astype(bf16)


def band(row):
    wide = jnp.broadcast_to(row, (256, 256))
    rolled = pltpu.roll(wide, 0, 1, stride=1, stride_axis=0)
    gap = lax.broadcasted_iota(jnp.int32, (256, 256), 0) - lax.broadcasted_iota(jnp.int32, (256, 256), 1)
    return jnp.where((gap <= 14) & (gap >= -14), rolled, 0.0).astype(bf16)


def inside_planes(start_ref, len_ref, first_orbital, first_plane, o, width):
    begin = start_ref[first_orbital + o] - first_plane
    plane = lax.broadcasted_iota(jnp.int32, (16, width), 0)
    return (plane >= begin) & (plane < begin + len_ref[first_orbital + o])


def fine_points(fine):
    spread = (
        lax.broadcasted_iota(jnp.int32, (16, 256), 1) // ZB == lax.broadcasted_iota(jnp.int32, (16, 256), 0)
    ).astype(bf16)
    return jnp.dot((fine > 0).astype(f32).astype(bf16), spread, preferred_element_type=f32)


def placed(rows, spot):
    taps = rows.shape[1]
    t = lax.broadcasted_iota(jnp.int32, (taps, 256), 0)
    lane = lax.broadcasted_iota(jnp.int32, (taps, 256), 1)
    return jnp.dot(rows, (lane == spot(t)).astype(bf16), preferred_element_type=f32)


def pack(wide, pack_ref, half):
    unit = eye(128)

    def step(j, _):
        row = half * 4096 + j
        both = jnp.concatenate([wide[pl.ds(row, 64, stride=64), :], wide[pl.ds(row + 32, 64, stride=64), :]], axis=0)
        turned_over = lax.dot_general(
            unit, both.astype(bf16), (((1,), (1,)), ((), ())), preferred_element_type=f32
        ).astype(bf16)
        for q in range(8):
            pack_ref[half * 8 + q, rows_at(j, 16), :] = turned_over[q * 16 : q * 16 + 16, :]
        return 0

    lax.fori_loop(0, 32, step, 0, unroll=4)


VM = pl.BlockSpec(memory_space=pltpu.VMEM)
HB = pl.BlockSpec(memory_space=pl.ANY)


def shape(dims, kind=bf16):
    return jax.ShapeDtypeStruct(dims, kind)


def plane_steps():
    return [(s, t) for s in range(4) for t in range(4) if s or t]


FAR_FIRST = (
    (2, 2), (0, 2), (2, 0), (1, 2), (3, 2), (2, 1), (2, 3), (1, 1), (3, 3), (3, 1), (1, 3), (0, 1), (0, 3), (1, 0), (3, 0),
)


GROUPS = ((0, 1024, 2, (0, 1)), (1024, 512, 1, (0, 2)), (1536, 512, 0, (1, 2)))


def remote(src, dst, ssem, rsem, to):
    return pltpu.make_async_remote_copy(
        src_ref=src, dst_ref=dst, send_sem=ssem, recv_sem=rsem, device_id=to, device_id_type=MESH
    )


class Group:
    def __init__(self, g, scale, w_ref, out_ref, h_in, h_sum, q_in, q_sum, f_in, f_sum, sems):
        self.g, self.scale = g, scale
        self.w, self.out, self.h_in, self.h_sum = w_ref, out_ref, h_in, h_sum
        self.q_in, self.q_sum, self.f_in, self.f_sum = q_in, q_sum, f_in, f_sum
        self.sems = sems
        self.col, self.width, self.axis, self.plane = GROUPS[g]
        self.cols = pl.ds(self.col, self.width)
        self.here = coords()
        z, x, y, core = self.here
        self.mate = at(z, x, y, 1 - core)
        self.keep = pl.multiple_of(core * 512, 512)
        self.give = pl.multiple_of(512 - core * 512, 512)
        self.sent = []

    def begin(self):
        s0, r0 = self.sems[0:2]
        rows = pl.ds(self.give, 512)
        self.copy0 = remote(self.w.at[rows, self.cols], self.h_in.at[:, self.cols], s0.at[self.g], r0.at[self.g], self.mate)
        self.copy0.start()

    def to_axis(self):
        s1, r1 = self.sems[2:4]
        self.copy0.wait()

        def add(i, _):
            rows = rows_at(i, 32)
            mine = pl.ds(pl.multiple_of(self.keep + i * 32, 32), 32)
            total = self.w[mine, self.cols].astype(f32) + self.h_in[rows, self.cols].astype(f32)
            self.h_sum[rows, self.cols] = total.astype(bf16)
            return 0

        lax.fori_loop(0, 16, add, 0)
        self.copies1 = []
        for s in (2, 1, 3):
            to = turned(self.here, self.axis, s)
            rows = pl.ds(pl.multiple_of(to[self.axis] * 128, 128), 128)
            c = remote(self.h_sum.at[rows, self.cols], self.q_in.at[s - 1], s1.at[self.g, s - 1], r1.at[self.g, s - 1], at(*to))
            c.start()
            self.copies1.append(c)
        self.sent += self.copies1

    def piece(self, pos):
        b = pos[self.plane[0]] * 4 + pos[self.plane[1]]
        half = self.width // 2
        return (b // 2) * 16, (b % 2) * half, half

    def to_plane(self):
        s2, r2 = self.sems[4:6]
        for c in self.copies1:
            c.wait_recv()
        base = pl.multiple_of(self.here[self.axis] * 128, 128)

        def add(i, _):
            rows = rows_at(i, 16)
            total = self.h_sum[pl.ds(pl.multiple_of(base + i * 16, 16), 16), self.cols].astype(f32)
            for s in range(3):
                total = total + self.q_in[s, rows, :].astype(f32)
            self.q_sum[rows, :] = total.astype(bf16)
            return 0

        lax.fori_loop(0, 8, add, 0)
        self.copies2 = []
        for n, (s, t) in enumerate(plane_steps()):
            to = turned(turned(self.here, self.plane[0], s), self.plane[1], t)
            row, col, half = self.piece(to)
            src = self.q_sum.at[pl.ds(pl.multiple_of(row, 16), 16), pl.ds(pl.multiple_of(col, 128), half)]
            c = remote(src, self.f_in.at[n], s2.at[self.g, n], r2.at[self.g, n], at(*to))
            c.start()
            self.copies2.append(c)
        self.sent += self.copies2

    def from_plane(self):
        t2, u2 = self.sems[6:8]
        for c in self.copies2:
            c.wait_recv()
        row, col, half = self.piece(self.here)
        total = self.q_sum[pl.ds(pl.multiple_of(row, 16), 16), pl.ds(pl.multiple_of(col, 128), half)].astype(f32)
        for n in range(15):
            total = total + self.f_in[n].astype(f32)
        self.f_sum[...] = (total * self.scale).astype(bf16)
        spot = self.out.at[
            pl.ds(pl.multiple_of(self.keep + self.here[self.axis] * 128 + row, 16), 16),
            pl.ds(pl.multiple_of(self.col + col, 128), half),
        ]
        self.copies3 = []
        for n, (s, t) in enumerate(plane_steps()):
            to = turned(turned(self.here, self.plane[0], s), self.plane[1], t)
            c = remote(self.f_sum, spot, t2.at[self.g, n], u2.at[self.g, n], at(*to))
            c.start()
            self.copies3.append(c)
        self.own = pltpu.make_async_copy(self.f_sum, spot, t2.at[self.g, 15])
        self.own.start()
        self.sent += self.copies3

    def from_axis(self):
        t1, u1 = self.sems[8:10]
        self.own.wait()
        for c in self.copies3:
            c.wait_recv()
        spot = self.out.at[pl.ds(pl.multiple_of(self.keep + self.here[self.axis] * 128, 128), 128), self.cols]
        self.copies4 = []
        for s in (2, 1, 3):
            c = remote(spot, spot, t1.at[self.g, s - 1], u1.at[self.g, s - 1], at(*turned(self.here, self.axis, s)))
            c.start()
            self.copies4.append(c)
        self.sent += self.copies4

    def to_mate(self):
        t0, u0 = self.sems[10:12]
        for c in self.copies4:
            c.wait_recv()
        spot = self.out.at[pl.ds(self.keep, 512), self.cols]
        self.copy5 = remote(spot, spot, t0.at[self.g], u0.at[self.g], self.mate)
        self.copy5.start()

    def finish(self):
        self.copy5.wait()
        for c in self.sent:
            c.wait_send()


def spread_copies(pack_ref, got_ref, send, recv):
    here = coords()
    me = here[0] * 4 + here[1]
    copies = []
    for n, (s, t) in enumerate(FAR_FIRST):
        to = turned(turned(here, 0, s), 1, t)
        copies.append((to[0], remote(pack_ref.at[to[0] * 4 + to[1]], got_ref.at[me], send.at[n], recv.at[n], at(*to))))
    return copies, (here[0], pltpu.make_async_copy(pack_ref.at[me], got_ref.at[me], send.at[15]))


def started(copy, chosen):
    @pl.when(chosen)
    def _():
        copy.start()


def mover():
    l = lax.broadcasted_iota(jnp.int32, (256, 256), 0)
    n = lax.broadcasted_iota(jnp.int32, (256, 256), 1)
    swapped = jnp.where((n >= 64) & (n < 128), n + 64, jnp.where((n >= 128) & (n < 192), n - 64, n))
    return (l == swapped).astype(bf16)


def main_kernel(
    scale, psi_hbm, start_hbm, len_hbm, fine_hbm, occ_hbm, taps_hbm, magic_hbm, ext_hbm, density_ref, trial_hbm, s_hbm,
    psi, start_ref, len_ref, fine_ref, occ_ref, taps, magic, ext_ref, sem_in, sem_psi,
    masked, values, part, pack_x, got, low, high, parts, wide, fine_on, weighted, bands, forward, across, pack_a, got_a,
    xt, a_t, trial, out, x_rows, w, h_in, h_sum, *rest,
):
    q_in, q_sum, f_in, f_sum = rest[0:3], rest[3:6], rest[6:9], rest[9:12]
    sems = rest[12:24]
    sd, rd, sh, rh, sx, rx, sa, ra, sem_out = rest[24:]
    here = coords()
    z, x, y, core = here
    orb, comp = lax.axis_index("orb"), lax.axis_index("comp")
    first_orbital, first_plane = orb * 64, comp * 16

    small = [
        pltpu.make_async_copy(src, dst, sem_in.at[n])
        for n, (src, dst) in enumerate(
            (
                (taps_hbm, taps), (magic_hbm, magic), (start_hbm, start_ref), (len_hbm, len_ref), (fine_hbm, fine_ref),
                (occ_hbm, occ_ref), (ext_hbm, ext_ref),
            )
        )
    ]
    for c in small:
        c.start()
    psi_copies = [
        pltpu.make_async_copy(psi_hbm.at[pl.ds(16 * n, 16)], psi.at[pl.ds(16 * n, 16)], sem_psi.at[n]) for n in range(4)
    ]
    for c in psi_copies:
        c.start()

    targets = [at(z, x, y, 1 - core), at(z, x, lax.rem(y + 3 + 2 * core, 4), 1 - core)]
    for a in (0, 1, 2):
        targets += [at(*turned(here, a, s)) for s in (1, 2, 3)]
    for a, b in ((0, 1), (0, 2), (1, 2)):
        targets += [at(*turned(turned(here, a, s), b, t)) for s in (1, 2, 3) for t in (1, 2, 3)]
    barrier = pltpu.get_barrier_semaphore()
    for t in targets:
        pl.semaphore_signal(barrier, inc=1, device_id=t, device_id_type=MESH)

    for c in small:
        c.wait()
    rows = []
    for e in range(4):
        rows.append(placed(taps[e], lambda t: lax.rem(270 - t, 256)))
    magic_rows = placed(magic[...], lambda t: lax.rem(263 - t, 256))
    adjoint_rows = placed(magic[...], lambda t: lax.rem(t + 249, 256))
    for d in range(4):
        for e in range(4):
            bands[d * 4 + e] = band(rows[e][d : d + 1])
        bands[16 + d] = band(adjoint_rows[d : d + 1])
        forward[d] = band(magic_rows[d : d + 1])
    spot = lax.rem(lax.broadcasted_iota(jnp.int32, (16, 256), 1), 48)
    edge = ((comp == 0) & (spot < 16)) | ((comp == 7) & (spot >= 32))
    for e in range(4):
        line = sum(placed(taps[e, d : d + 1], lambda t, d=d: t + (d * 48 + 2)) for d in range(4))
        rolled = pltpu.roll(jnp.broadcast_to(line, (16, 256)), 0, 1, stride=1, stride_axis=0)
        across[pl.ds(e * 16, 16), :] = jnp.where(edge, 0.0, rolled).astype(bf16)

    fine_on[...] = fine_points(fine_ref[...])
    fine = fine_on[...] > 0.5
    for n in range(4):
        psi_copies[n].wait()

        def mask(o, _):
            inside = inside_planes(start_ref, len_ref, first_orbital, first_plane, o, 256)
            for c in range(4):
                on = inside if c == 0 else inside & fine
                value = jnp.where(on, psi[o, c].astype(f32), 0.0)
                masked[o, c] = value.astype(bf16)
                spots = pl.ds(pl.multiple_of(o * 64 + c * 16, 16), 16)
                wide[spots, :] = value[:, :128]
                wide[pl.ds(pl.multiple_of(4096 + o * 64 + c * 16, 16), 16), :] = value[:, 128:]
            return 0

        lax.fori_loop(16 * n, 16 * n + 16, mask, 0, unroll=2)
    def block(i, total):
        seen = jnp.zeros((256, 256), f32)
        for d in range(4):
            seen = seen + jnp.dot(masked[rows_at(i, 16), d].reshape(256, 256), forward[d], preferred_element_type=f32)
        for n in range(16):
            one = seen[n * 16 : n * 16 + 16]
            values[i * 16 + n] = one
            total = total + occ_ref[first_orbital + i * 16 + n].astype(f32) * (one * one)
        return total

    part[...] = lax.fori_loop(0, 4, block, jnp.zeros((16, 256), f32))
    halves = (lax.rem(x, 2), 1 - lax.rem(x, 2))
    spread_x, own_x = spread_copies(pack_x, got, sx, rx)
    spread_a, own_a = spread_copies(pack_a, got_a, sa, ra)
    pack(wide, pack_x, halves[0])
    pl.semaphore_wait(barrier, len(targets))

    halo_copies = []
    for n, h in enumerate(halves):
        lanes = pl.ds(pl.multiple_of(128 * h, 128), 128)
        source = masked.at[:, :, :, lanes]
        for k, (ref, turn) in enumerate(((low, 1), (high, 7))):
            halo_copies.append(
                remote(
                    source, ref.at[:, :, :, lanes], sh.at[2 * n + k], rh.at[2 * n + k],
                    {"orb": orb, "comp": lax.rem(comp + turn, 8)},
                )
            )
    for c in halo_copies:
        c.start()

    density_copies = []
    for n, (s, t) in enumerate(FAR_FIRST):
        to = turned(turned(here, 0, s), 1, t)
        density_copies.append(remote(part, parts.at[n], sd.at[n], rd.at[n], at(*to)))
    for c in density_copies:
        c.start()

    for to_z, c in spread_x + [own_x]:
        started(c, lax.div(to_z, 2) == halves[0])
    pack(wide, pack_x, halves[1])
    for to_z, c in spread_x + [own_x]:
        started(c, lax.div(to_z, 2) == halves[1])

    density = part[...]
    for n in range(15):
        density_copies[n].wait_recv()
        density = density + parts[n]
    density_ref[...] = pltpu.roll(density, 256 - orb * 16, 1)[:, :16]
    potential = ext_ref[...] - xc_factor * jnp.exp(jnp.log(density) * (1.0 / 3.0))

    def weigh(o, _):
        weighted[o] = (potential * values[o]).astype(bf16)
        return 0

    lax.fori_loop(0, 64, weigh, 0, unroll=4)

    def along(i, _):
        for e in range(4):
            total = jnp.dot(weighted[rows_at(i, 16)].reshape(256, 256), bands[16 + e], preferred_element_type=f32)
            for d in range(4):
                total = total + jnp.dot(
                    masked[rows_at(i, 16), d].reshape(256, 256), bands[d * 4 + e], preferred_element_type=f32
                )
            for n in range(16):
                spots = pl.ds(pl.multiple_of((i * 16 + n) * 64 + e * 16, 16), 16)
                wide[spots, :] = total[n * 16 : n * 16 + 16, :128]
                spots = pl.ds(pl.multiple_of(4096 + (i * 16 + n) * 64 + e * 16, 16), 16)
                wide[spots, :] = total[n * 16 : n * 16 + 16, 128:]
        return 0

    lax.fori_loop(0, 4, along, 0)

    for n, h in enumerate(halves):
        for c in halo_copies[2 * n : 2 * n + 2]:
            c.wait_recv()
        lanes = pl.ds(pl.multiple_of(128 * h, 128), 128)
        fine_half = fine_on[:, lanes] > 0.5

        def cross(i, _, h=h, lanes=lanes, fine_half=fine_half):
            o = 2 * i
            window = jnp.concatenate(
                [
                    jnp.concatenate([ref[o, d, :, lanes], ref[o + 1, d, :, lanes]], axis=1)
                    for d in range(4)
                    for ref in (low, masked, high)
                ],
                axis=0,
            )
            summed = jnp.dot(across[:, :192], window, preferred_element_type=f32)
            for k in range(2):
                inside = inside_planes(start_ref, len_ref, first_orbital, first_plane, o + k, 128)
                for e in range(4):
                    on = inside if e == 0 else inside & fine_half
                    spots = pl.ds(pl.multiple_of(h * 4096 + (o + k) * 64 + e * 16, 16), 16)
                    term = summed[e * 16 : e * 16 + 16, 128 * k : 128 * k + 128]
                    wide[spots, :] = jnp.where(on, term + wide[spots, :], 0.0)
            return 0

        lax.fori_loop(0, 32, cross, 0, unroll=4)
        pack(wide, pack_a, h)
        for to_z, c in spread_a + [own_a]:
            started(c, lax.div(to_z, 2) == h)

    move = mover()
    own_x[1].wait()
    for _, c in spread_x:
        c.wait_recv()

    def unpack_x(m, _):
        pair = jnp.concatenate([got[2 * m], got[2 * m + 1]], axis=1)
        turned_back = jnp.dot(pair, move, preferred_element_type=f32).astype(bf16)
        spots = pl.ds(pl.multiple_of(128 * m, 128), 128)
        xt[0:512, spots] = turned_back[:, :128]
        xt[512:1024, spots] = turned_back[:, 128:]
        across_rows = lax.dot_general(move, pair, (((1,), (1,)), ((), ())), preferred_element_type=f32).astype(bf16)
        x_rows[spots, 0:512] = across_rows[:128]
        x_rows[spots, 512:1024] = across_rows[128:]
        return 0

    lax.fori_loop(0, 8, unpack_x, 0)
    groups = [Group(g, scale, w, out, h_in, h_sum, q_in[g], q_sum[g], f_in[g], f_sum[g], sems) for g in range(3)]
    overlap, first, second = groups

    keep, give = pl.multiple_of(core * 512, 512), pl.multiple_of(512 - core * 512, 512)

    def products(other, col, first_row):
        def step(i, _):
            spots = pl.ds(pl.multiple_of(first_row + i * 256, 256), 256)
            w[spots, col : col + 1024] = jnp.dot(x_rows[spots, :], other[...], preferred_element_type=f32).astype(bf16)
            return 0

        lax.fori_loop(0, 2, step, 0)

    products(xt, 0, give)
    overlap.begin()
    products(xt, 0, keep)
    overlap.to_axis()
    overlap.to_plane()
    own_a[1].wait()
    for _, c in spread_a:
        c.wait_recv()

    def unpack_a(m, _):
        pair = jnp.concatenate([got_a[2 * m], got_a[2 * m + 1]], axis=1)
        turned_back = jnp.dot(pair, move, preferred_element_type=f32).astype(bf16)
        spots = pl.ds(pl.multiple_of(128 * m, 128), 128)
        a_t[0:512, spots] = turned_back[:, :128]
        a_t[512:1024, spots] = turned_back[:, 128:]
        return 0

    lax.fori_loop(0, 8, unpack_a, 0)
    products(a_t, 1024, give)
    first.begin()
    second.begin()
    products(a_t, 1024, keep)
    first.to_axis()
    second.to_axis()
    first.to_plane()
    second.to_plane()
    overlap.from_plane()
    first.from_plane()
    second.from_plane()
    first.from_axis()
    second.from_axis()
    overlap.from_axis()
    first.to_mate()
    second.to_mate()
    first.finish()
    second.finish()
    for n in range(4):
        spots = pl.ds(256 * n, 256)
        mine = xt[spots, :]
        gradient = a_t[spots, :].astype(f32) - jnp.dot(mine, out[:, 1024:2048], preferred_element_type=f32)
        trial[spots, :] = (mine.astype(f32) - step_length * gradient).astype(bf16)
    trial_copy = pltpu.make_async_copy(trial, trial_hbm, sem_out.at[0])
    trial_copy.start()
    overlap.to_mate()
    for c in density_copies + halo_copies + [c for _, c in spread_x + spread_a]:
        c.wait_send()
    overlap.finish()
    s_copy = pltpu.make_async_copy(out.at[:, pl.ds(0, 1024)], s_hbm, sem_out.at[1])
    s_copy.start()
    trial_copy.wait()
    s_copy.wait()


def last_kernel(trial_hbm, s_hbm, part_hbm, next_hbm, density_hbm, trial, s_all, part, following, sems):
    copies = [pltpu.make_async_copy(s_hbm, s_all, sems.at[0])]
    for n in range(4):
        rows = pl.ds(256 * n, 256)
        copies.append(pltpu.make_async_copy(trial_hbm.at[rows], trial.at[rows], sems.at[1 + n]))
    copies.append(pltpu.make_async_copy(part_hbm, part, sems.at[5]))
    for c in copies:
        c.start()
    copies[5].wait()
    done = [pltpu.make_async_copy(part, density_hbm, sems.at[6])]
    done[0].start()
    copies[0].wait()
    for n in range(4):
        rows = pl.ds(256 * n, 256)
        copies[1 + n].wait()
        now = trial[rows, :]
        stepped = 1.5 * now.astype(f32) - 0.5 * jnp.dot(now, s_all[...], preferred_element_type=f32)
        following[rows, :] = stepped.astype(bf16)
        done.append(pltpu.make_async_copy(following.at[rows], next_hbm.at[rows], sems.at[7 + n]))
        done[-1].start()
    for c in done:
        c.wait()


def last_step(trial, s_all, part):
    vm = pltpu.VMEM
    square = vm((1024, 1024), bf16)
    return pl.pallas_call(
        last_kernel,
        out_shape=(shape((1024, 1024)), shape((16, 16), f32)),
        in_specs=[HB] * 3,
        out_specs=(HB,) * 2,
        scratch_shapes=[square, square, vm((16, 16), f32), square, pltpu.SemaphoreType.DMA((11,))],
        compiler_params=pltpu.CompilerParams(vmem_limit_bytes=VMEM_MAIN),
        name="last",
    )(trial, s_all, part)


def main_step(scale, *args):
    dma = pltpu.SemaphoreType.DMA
    vm = pltpu.VMEM
    sm = pltpu.SMEM
    widths = [g[1] for g in GROUPS]
    spread_buffer = vm((16, 512, 128), bf16)
    square = vm((1024, 1024), bf16)
    orbitals = vm((64, 4, 16, 256), bf16)
    return pl.pallas_call(
        functools.partial(main_kernel, scale),
        out_shape=(shape((16, 16), f32), shape((1024, 1024)), shape((1024, 1024))),
        in_specs=[HB] * 8,
        out_specs=(VM, HB, HB),
        scratch_shapes=[orbitals, sm((1024,), jnp.int32), sm((1024,), jnp.int32), vm((16, 16), jnp.int32)]
        + [sm((1024,), jnp.int32), vm((4, 4, 29), bf16), vm((4, 16), bf16), vm((16, 256), f32), dma((7,)), dma((4,))]
        + [orbitals, vm((64, 16, 256), f32), vm((16, 256), f32), spread_buffer, spread_buffer, orbitals, orbitals]
        + [vm((15, 16, 256), f32), vm((8192, 128), f32), vm((16, 256), f32), vm((64, 16, 256), bf16)]
        + [vm((20, 256, 256), bf16), vm((4, 256, 256), bf16), vm((64, 256), bf16), spread_buffer, spread_buffer]
        + [square, square, square, vm((1024, 2048), bf16), square]
        + [vm((1024, 2048), bf16), vm((512, 2048), bf16), vm((512, 2048), bf16)]
        + [vm((3, 128, n), bf16) for n in widths]
        + [vm((128, n), bf16) for n in widths]
        + [vm((15, 16, n // 2), bf16) for n in widths]
        + [vm((16, n // 2), bf16) for n in widths]
        + [dma((3,)), dma((3,)), dma((3, 3)), dma((3, 3)), dma((3, 15)), dma((3, 15))]
        + [dma((3, 16)), dma((3, 15)), dma((3, 3)), dma((3, 3)), dma((3,)), dma((3,))]
        + [dma((15,)), dma((15,)), dma((4,)), dma((4,)), dma((16,)), dma((15,)), dma((16,)), dma((15,)), dma((2,))],
        compiler_params=pltpu.CompilerParams(collective_id=3, has_side_effects=True, vmem_limit_bytes=VMEM_MAIN),
        name="main",
    )(*args)


VMEM_MAIN = 58 << 20


def local(psi, region_start, region_len, fine_mask, occupation, kinetic_taps, magic_taps, external):
    density, trial, intersection = main_step(
        1.0 / 32768, psi, region_start, region_len, fine_mask, occupation,
        jnp.transpose(kinetic_taps, (1, 2, 0)), jnp.transpose(magic_taps), external,
    )
    following, density = last_step(trial, intersection, density)
    return (density, jnp.transpose(following.reshape(4, 16, 16, 1024), (3, 0, 1, 2)))


def solution(mesh):
    return jax.shard_map(
        local,
        mesh=mesh,
        in_specs=(
            P("orb", None, "comp", None),
            P(),
            P(),
            P("comp", None),
            P(),
            P(),
            P(),
            P("comp", None),
        ),
        out_specs=(P("comp", "orb"), P(None, None, "comp", "orb")),
        check_vma=False,
    )
```

time: 158 us -> 123 us (0.78)
  Pallas kernels: 135 us -> 122 us
  local copies, waits for them, and re-layouts: 11.4 us -> 0 us
  matrix products: 8.71 us -> 0 us
    pallas_call x1, Pallas kernels: 128 us -> 116 us  [main_step(): pl.pallas_call(functools.partial(main_kernel, scale), out_shape=(shape((1...]
    unnamed x28 -> x0, local copies, waits for them, and re-layouts: 9.82 us -> none
    dot_general x2 -> x0, matrix products: 8.71 us -> none  [the longest x1 4.69 us: local(): jnp.dot(masked_k, lagrange_round, preferred_element_type=f32)]
where the time goes in v2:
time: 123 us; the launch traced here: 122 us
  Pallas kernels  122 us (99%)
    pallas_call x1, Pallas kernels, main_step(): pl.pallas_call(functools.partial(main_kernel, scale), out_shape=(shape((1...  116 us
    pallas_call x1, Pallas kernels, last_step(): pl.pallas_call(last_kernel, out_shape=(shape((1024, 1024)), shape((16, 16...  5.75 us

profile of v2, /device:TPU:1, one launch (start us, length us, event | category | flops | bytes accessed | tf_op | source)
XLA Modules:
  0.0 122.4 jit_solution(16308530607700885783)
XLA Ops:
  0.6 115.8 %main.1 = (f32[16,16]{1,0:T(8,128)}, bf16[1024,1024]{1,0:T(8,128)(2,1)}, bf16[1024,1024]{1,0:T(8,128)(2,1)}) custom-call(bf16[64,4,16,256]{3,2,1,0:T(8,128)(2,1)} %psi_hbm.1, s32[1024]{0:T(1024)} %start_hbm.1, s32[1024]{0:T(1024)} %len_hbm.1, s32[16,16]{1,0:T(8,128)} %fine_hbm.1, s32[1024]{0:T(1024)} %occ_hbm.1, bf16[4,4,29]{2,1,0:T(4,128)(2,1)} %bitcast.5, ...), custom_call_target="tpu_custom_call" | custom-call | tf_op jit(solution)/shard_map/main/pallas_call | solution.py:566
  116.5 5.8 %last.1 = (bf16[1024,1024]{1,0:T(8,128)(2,1)}, f32[16,16]{1,0:T(8,128)}) custom-call(bf16[1024,1024]{1,0:T(8,128)(2,1)} %get-tuple-element.7.trial_hbm, bf16[1024,1024]{1,0:T(8,128)(2,1)} %get-tuple-element.8.s_hbm, f32[16,16]{1,0:T(8,128)} %get-tuple-element.9.part_hbm), custom_call_target="tpu_custom_call" | custom-call | tf_op jit(solution)/shard_map/last/pallas_call | solution.py:547

commit v3 on v2

--- a/solution.py
+++ b/solution.py
@@ -100,7 +100,10 @@
 )
 
 
-GROUPS = ((0, 1024, 2, (0, 1)), (1024, 512, 1, (0, 2)), (1536, 512, 0, (1, 2)))
+GROUPS = (
+    (0, 512, 2, (0, 1)), (512, 512, 2, (0, 1)),
+    (1024, 256, 1, (0, 2)), (1280, 256, 0, (1, 2)), (1536, 256, 1, (0, 2)), (1792, 256, 0, (1, 2)),
+)
 
 
 def remote(src, dst, ssem, rsem, to):
@@ -110,6 +113,16 @@
 
 
 class Group:
+    def owners(self, body):
+        if self.g == 0:
+            pl.when(self.here[3] == 0)(body)
+        else:
+            body()
+
+    def others(self, body):
+        if self.g == 0:
+            pl.when(self.here[3] == 1)(body)
+
     def __init__(self, g, scale, w_ref, out_ref, h_in, h_sum, q_in, q_sum, f_in, f_sum, sems):
         self.g, self.scale = g, scale
         self.w, self.out, self.h_in, self.h_sum = w_ref, out_ref, h_in, h_sum
@@ -117,6 +130,8 @@
         self.sems = sems
         self.col, self.width, self.axis, self.plane = GROUPS[g]
         self.cols = pl.ds(self.col, self.width)
+        self.out_col = self.col if g < 2 else self.col - 1024
+        self.out_cols = pl.ds(self.out_col, self.width)
         self.here = coords()
         z, x, y, core = self.here
         self.mate = at(z, x, y, 1 - core)
@@ -128,11 +143,13 @@
         s0, r0 = self.sems[0:2]
         rows = pl.ds(self.give, 512)
         self.copy0 = remote(self.w.at[rows, self.cols], self.h_in.at[:, self.cols], s0.at[self.g], r0.at[self.g], self.mate)
-        self.copy0.start()
+        if self.g == 0:
+            self.others(self.copy0.start)
+        else:
+            self.copy0.start()
 
     def to_axis(self):
         s1, r1 = self.sems[2:4]
-        self.copy0.wait()
 
         def add(i, _):
             rows = rows_at(i, 32)
@@ -141,15 +158,25 @@
             self.h_sum[rows, self.cols] = total.astype(bf16)
             return 0
 
-        lax.fori_loop(0, 16, add, 0)
         self.copies1 = []
         for s in (2, 1, 3):
             to = turned(self.here, self.axis, s)
             rows = pl.ds(pl.multiple_of(to[self.axis] * 128, 128), 128)
             c = remote(self.h_sum.at[rows, self.cols], self.q_in.at[s - 1], s1.at[self.g, s - 1], r1.at[self.g, s - 1], at(*to))
-            c.start()
             self.copies1.append(c)
         self.sent += self.copies1
+
+        def body():
+            if self.g:
+                self.copy0.wait()
+            else:
+                self.copy0.wait_recv()
+            lax.fori_loop(0, 16, add, 0)
+            for c in self.copies1:
+                c.start()
+
+        self.others(self.copy0.wait_send)
+        self.owners(body)
 
     def piece(self, pos):
         b = pos[self.plane[0]] * 4 + pos[self.plane[1]]
@@ -158,8 +185,6 @@
 
     def to_plane(self):
         s2, r2 = self.sems[4:6]
-        for c in self.copies1:
-            c.wait_recv()
         base = pl.multiple_of(self.here[self.axis] * 128, 128)
 
         def add(i, _):
@@ -170,65 +195,94 @@
             self.q_sum[rows, :] = total.astype(bf16)
             return 0
 
-        lax.fori_loop(0, 8, add, 0)
         self.copies2 = []
         for n, (s, t) in enumerate(plane_steps()):
             to = turned(turned(self.here, self.plane[0], s), self.plane[1], t)
             row, col, half = self.piece(to)
             src = self.q_sum.at[pl.ds(pl.multiple_of(row, 16), 16), pl.ds(pl.multiple_of(col, 128), half)]
             c = remote(src, self.f_in.at[n], s2.at[self.g, n], r2.at[self.g, n], at(*to))
-            c.start()
             self.copies2.append(c)
         self.sent += self.copies2
 
+        def body():
+            for c in self.copies1:
+                c.wait_recv()
+            lax.fori_loop(0, 8, add, 0)
+            for c in self.copies2:
+                c.start()
+
+        self.owners(body)
+
     def from_plane(self):
         t2, u2 = self.sems[6:8]
-        for c in self.copies2:
-            c.wait_recv()
         row, col, half = self.piece(self.here)
-        total = self.q_sum[pl.ds(pl.multiple_of(row, 16), 16), pl.ds(pl.multiple_of(col, 128), half)].astype(f32)
-        for n in range(15):
-            total = total + self.f_in[n].astype(f32)
-        self.f_sum[...] = (total * self.scale).astype(bf16)
+        own_piece = (pl.ds(pl.multiple_of(row, 16), 16), pl.ds(pl.multiple_of(col, 128), half))
         spot = self.out.at[
             pl.ds(pl.multiple_of(self.keep + self.here[self.axis] * 128 + row, 16), 16),
-            pl.ds(pl.multiple_of(self.col + col, 128), half),
+            pl.ds(pl.multiple_of(self.out_col + col, 128), half),
         ]
         self.copies3 = []
         for n, (s, t) in enumerate(plane_steps()):
             to = turned(turned(self.here, self.plane[0], s), self.plane[1], t)
             c = remote(self.f_sum, spot, t2.at[self.g, n], u2.at[self.g, n], at(*to))
-            c.start()
             self.copies3.append(c)
         self.own = pltpu.make_async_copy(self.f_sum, spot, t2.at[self.g, 15])
-        self.own.start()
         self.sent += self.copies3
+
+        def body():
+            for c in self.copies2:
+                c.wait_recv()
+            total = self.q_sum[own_piece].astype(f32)
+            for n in range(15):
+                total = total + self.f_in[n].astype(f32)
+            self.f_sum[...] = (total * self.scale).astype(bf16)
+            for c in self.copies3:
+                c.start()
+            self.own.start()
+
+        self.owners(body)
 
     def from_axis(self):
         t1, u1 = self.sems[8:10]
-        self.own.wait()
-        for c in self.copies3:
-            c.wait_recv()
-        spot = self.out.at[pl.ds(pl.multiple_of(self.keep + self.here[self.axis] * 128, 128), 128), self.cols]
+        spot = self.out.at[pl.ds(pl.multiple_of(self.keep + self.here[self.axis] * 128, 128), 128), self.out_cols]
         self.copies4 = []
         for s in (2, 1, 3):
             c = remote(spot, spot, t1.at[self.g, s - 1], u1.at[self.g, s - 1], at(*turned(self.here, self.axis, s)))
-            c.start()
             self.copies4.append(c)
         self.sent += self.copies4
 
+        def body():
+            self.own.wait()
+            for c in self.copies3:
+                c.wait_recv()
+            for c in self.copies4:
+                c.start()
+
+        self.owners(body)
+
     def to_mate(self):
         t0, u0 = self.sems[10:12]
-        for c in self.copies4:
-            c.wait_recv()
-        spot = self.out.at[pl.ds(self.keep, 512), self.cols]
+        spot = self.out.at[pl.ds(self.keep, 512), self.out_cols]
         self.copy5 = remote(spot, spot, t0.at[self.g], u0.at[self.g], self.mate)
-        self.copy5.start()
+
+        def body():
+            for c in self.copies4:
+                c.wait_recv()
+            self.copy5.start()
+
+        self.owners(body)
 
     def finish(self):
-        self.copy5.wait()
-        for c in self.sent:
-            c.wait_send()
+        def body():
+            if self.g:
+                self.copy5.wait()
+            else:
+                self.copy5.wait_send()
+            for c in self.sent:
+                c.wait_send()
+
+        self.others(self.copy5.wait_recv)
+        self.owners(body)
 
 
 def spread_copies(pack_ref, got_ref, send, recv):
@@ -255,14 +309,14 @@
 
 
 def main_kernel(
-    scale, psi_hbm, start_hbm, len_hbm, fine_hbm, occ_hbm, taps_hbm, magic_hbm, ext_hbm, density_ref, trial_hbm, s_hbm,
+    scale, psi_hbm, start_hbm, len_hbm, fine_hbm, occ_hbm, taps_hbm, magic_hbm, ext_hbm, density_ref, trial, s_ref,
     psi, start_ref, len_ref, fine_ref, occ_ref, taps, magic, ext_ref, sem_in, sem_psi,
     masked, values, part, pack_x, got, low, high, parts, wide, fine_on, weighted, bands, forward, across, pack_a, got_a,
-    xt, a_t, trial, out, x_rows, w, h_in, h_sum, *rest,
+    xt, a_t, out, x_rows, w, h_in, h_sum, *rest,
 ):
-    q_in, q_sum, f_in, f_sum = rest[0:3], rest[3:6], rest[6:9], rest[9:12]
-    sems = rest[12:24]
-    sd, rd, sh, rh, sx, rx, sa, ra, sem_out = rest[24:]
+    q_in, q_sum, f_in, f_sum = rest[0:6], rest[6:12], rest[12:18], rest[18:24]
+    sems = rest[24:36]
+    sd, rd, sh, rh, sx, rx, sa, ra = rest[36:]
     here = coords()
     z, x, y, core = here
     orb, comp = lax.axis_index("orb"), lax.axis_index("comp")
@@ -348,13 +402,13 @@
     pl.semaphore_wait(barrier, len(targets))
 
     halo_copies = []
-    for n, h in enumerate(halves):
-        lanes = pl.ds(pl.multiple_of(128 * h, 128), 128)
-        source = masked.at[:, :, :, lanes]
+    halo_parts = ((0, 0, 64), (1, 0, 32), (1, 32, 32))
+    for n, (m, o, count) in enumerate(halo_parts):
+        spot = (pl.ds(o, count), slice(None), slice(None), pl.ds(pl.multiple_of(128 * halves[m], 128), 128))
         for k, (ref, turn) in enumerate(((low, 1), (high, 7))):
             halo_copies.append(
                 remote(
-                    source, ref.at[:, :, :, lanes], sh.at[2 * n + k], rh.at[2 * n + k],
+                    masked.at[spot], ref.at[spot], sh.at[2 * n + k], rh.at[2 * n + k],
                     {"orb": orb, "comp": lax.rem(comp + turn, 8)},
                 )
             )
@@ -404,8 +458,6 @@
     lax.fori_loop(0, 4, along, 0)
 
     for n, h in enumerate(halves):
-        for c in halo_copies[2 * n : 2 * n + 2]:
-            c.wait_recv()
         lanes = pl.ds(pl.multiple_of(128 * h, 128), 128)
         fine_half = fine_on[:, lanes] > 0.5
 
@@ -429,7 +481,11 @@
                     wide[spots, :] = jnp.where(on, term + wide[spots, :], 0.0)
             return 0
 
-        lax.fori_loop(0, 32, cross, 0, unroll=4)
+        for p, (m, o, count) in enumerate(halo_parts):
+            if m == n:
+                for c in halo_copies[2 * p : 2 * p + 2]:
+                    c.wait_recv()
+                lax.fori_loop(o // 2, (o + count) // 2, cross, 0, unroll=4)
         pack(wide, pack_a, h)
         for to_z, c in spread_a + [own_a]:
             started(c, lax.div(to_z, 2) == h)
@@ -451,8 +507,8 @@
         return 0
 
     lax.fori_loop(0, 8, unpack_x, 0)
-    groups = [Group(g, scale, w, out, h_in, h_sum, q_in[g], q_sum[g], f_in[g], f_sum[g], sems) for g in range(3)]
-    overlap, first, second = groups
+    groups = [Group(g, scale, w, out if g > 1 else s_ref, h_in, h_sum, q_in[g], q_sum[g], f_in[g], f_sum[g], sems) for g in range(6)]
+    corner, overlap = groups[:2]
 
     keep, give = pl.multiple_of(core * 512, 512), pl.multiple_of(512 - core * 512, 512)
 
@@ -465,92 +521,92 @@
         lax.fori_loop(0, 2, step, 0)
 
     products(xt, 0, give)
+    corner.begin()
     overlap.begin()
     products(xt, 0, keep)
+    corner.to_axis()
     overlap.to_axis()
+    corner.to_plane()
     overlap.to_plane()
-    own_a[1].wait()
-    for _, c in spread_a:
-        c.wait_recv()
-
-    def unpack_a(m, _):
-        pair = jnp.concatenate([got_a[2 * m], got_a[2 * m + 1]], axis=1)
-        turned_back = jnp.dot(pair, move, preferred_element_type=f32).astype(bf16)
-        spots = pl.ds(pl.multiple_of(128 * m, 128), 128)
-        a_t[0:512, spots] = turned_back[:, :128]
-        a_t[512:1024, spots] = turned_back[:, 128:]
-        return 0
-
-    lax.fori_loop(0, 8, unpack_a, 0)
+    for s in (2, 1, 3, 0):
+        for n, step in enumerate(FAR_FIRST):
+            if step[0] == s:
+                spread_a[n][1].wait_recv()
+        if s == 0:
+            own_a[1].wait()
+        source_z = lax.rem(z + 4 - s, 4)
+        for k in range(2):
+            m = 2 * source_z + k
+            pair = jnp.concatenate([got_a[2 * m], got_a[2 * m + 1]], axis=1)
+            turned_back = jnp.dot(pair, move, preferred_element_type=f32).astype(bf16)
+            spots = pl.ds(pl.multiple_of(128 * m, 128), 128)
+            a_t[0:512, spots] = turned_back[:, :128]
+            a_t[512:1024, spots] = turned_back[:, 128:]
     products(a_t, 1024, give)
-    first.begin()
-    second.begin()
+    for group in groups[2:]:
+        group.begin()
     products(a_t, 1024, keep)
-    first.to_axis()
-    second.to_axis()
-    first.to_plane()
-    second.to_plane()
+    for group in groups[2:]:
+        group.to_axis()
+    for group in groups[2:4]:
+        group.to_plane()
+    corner.from_plane()
     overlap.from_plane()
-    first.from_plane()
-    second.from_plane()
-    first.from_axis()
-    second.from_axis()
+    for group in groups[4:]:
+        group.to_plane()
+    for group in groups[2:]:
+        group.from_plane()
+    for group in groups[2:4]:
+        group.from_axis()
+    corner.from_axis()
     overlap.from_axis()
-    first.to_mate()
-    second.to_mate()
-    first.finish()
-    second.finish()
+    for group in groups[4:]:
+        group.from_axis()
+    for group in groups[2:]:
+        group.to_mate()
+    for group in groups[2:]:
+        group.finish()
+    corner.to_mate()
+    overlap.to_mate()
     for n in range(4):
         spots = pl.ds(256 * n, 256)
         mine = xt[spots, :]
-        gradient = a_t[spots, :].astype(f32) - jnp.dot(mine, out[:, 1024:2048], preferred_element_type=f32)
+        gradient = a_t[spots, :].astype(f32) - jnp.dot(mine, out[...], preferred_element_type=f32)
         trial[spots, :] = (mine.astype(f32) - step_length * gradient).astype(bf16)
-    trial_copy = pltpu.make_async_copy(trial, trial_hbm, sem_out.at[0])
-    trial_copy.start()
-    overlap.to_mate()
     for c in density_copies + halo_copies + [c for _, c in spread_x + spread_a]:
         c.wait_send()
+    corner.finish()
     overlap.finish()
-    s_copy = pltpu.make_async_copy(out.at[:, pl.ds(0, 1024)], s_hbm, sem_out.at[1])
-    s_copy.start()
-    trial_copy.wait()
-    s_copy.wait()
-
-
-def last_kernel(trial_hbm, s_hbm, part_hbm, next_hbm, density_hbm, trial, s_all, part, following, sems):
-    copies = [pltpu.make_async_copy(s_hbm, s_all, sems.at[0])]
+
+
+def last_kernel(trial, s_all, part, next_hbm, density, following, sems):
+    density[...] = part[...]
+    done = []
     for n in range(4):
         rows = pl.ds(256 * n, 256)
-        copies.append(pltpu.make_async_copy(trial_hbm.at[rows], trial.at[rows], sems.at[1 + n]))
-    copies.append(pltpu.make_async_copy(part_hbm, part, sems.at[5]))
-    for c in copies:
-        c.start()
-    copies[5].wait()
-    done = [pltpu.make_async_copy(part, density_hbm, sems.at[6])]
-    done[0].start()
-    copies[0].wait()
-    for n in range(4):
-        rows = pl.ds(256 * n, 256)
-        copies[1 + n].wait()
-        now = trial[rows, :]
-        stepped = 1.5 * now.astype(f32) - 0.5 * jnp.dot(now, s_all[...], preferred_element_type=f32)
-        following[rows, :] = stepped.astype(bf16)
-        done.append(pltpu.make_async_copy(following.at[rows], next_hbm.at[rows], sems.at[7 + n]))
+        one, two = trial[rows, 0:512], trial[rows, 512:1024]
+        left = jnp.dot(one, s_all[0:512, 0:512], preferred_element_type=f32) + lax.dot_general(
+            two, s_all[0:512, 512:1024], (((1,), (1,)), ((), ())), preferred_element_type=f32
+        )
+        right = jnp.dot(one, s_all[0:512, 512:1024], preferred_element_type=f32) + jnp.dot(
+            two, s_all[512:1024, 512:1024], preferred_element_type=f32
+        )
+        following[rows, 0:512] = (1.5 * one.astype(f32) - 0.5 * left).astype(bf16)
+        following[rows, 512:1024] = (1.5 * two.astype(f32) - 0.5 * right).astype(bf16)
+        done.append(pltpu.make_async_copy(following.at[rows], next_hbm.at[rows], sems.at[n]))
         done[-1].start()
     for c in done:
         c.wait()
 
 
 def last_step(trial, s_all, part):
-    vm = pltpu.VMEM
-    square = vm((1024, 1024), bf16)
     return pl.pallas_call(
         last_kernel,
         out_shape=(shape((1024, 1024)), shape((16, 16), f32)),
-        in_specs=[HB] * 3,
-        out_specs=(HB,) * 2,
-        scratch_shapes=[square, square, vm((16, 16), f32), square, pltpu.SemaphoreType.DMA((11,))],
-        compiler_params=pltpu.CompilerParams(vmem_limit_bytes=VMEM_MAIN),
+        in_specs=[VM] * 3,
+        out_specs=(pl.BlockSpec(memory_space=pltpu.HBM), VM),
+        scratch_shapes=[pltpu.VMEM((1024, 1024), bf16), pltpu.SemaphoreType.DMA((4,))],
+        compiler_params=pltpu.CompilerParams(vmem_limit_bytes=24 << 20),
         name="last",
     )(trial, s_all, part)
 
@@ -566,28 +622,28 @@
     return pl.pallas_call(
         functools.partial(main_kernel, scale),
         out_shape=(shape((16, 16), f32), shape((1024, 1024)), shape((1024, 1024))),
-        in_specs=[HB] * 8,
-        out_specs=(VM, HB, HB),
+        in_specs=[pl.BlockSpec(memory_space=pltpu.HBM)] * 8,
+        out_specs=(VM,) * 3,
         scratch_shapes=[orbitals, sm((1024,), jnp.int32), sm((1024,), jnp.int32), vm((16, 16), jnp.int32)]
         + [sm((1024,), jnp.int32), vm((4, 4, 29), bf16), vm((4, 16), bf16), vm((16, 256), f32), dma((7,)), dma((4,))]
         + [orbitals, vm((64, 16, 256), f32), vm((16, 256), f32), spread_buffer, spread_buffer, orbitals, orbitals]
         + [vm((15, 16, 256), f32), vm((8192, 128), f32), vm((16, 256), f32), vm((64, 16, 256), bf16)]
         + [vm((20, 256, 256), bf16), vm((4, 256, 256), bf16), vm((64, 256), bf16), spread_buffer, spread_buffer]
-        + [square, square, square, vm((1024, 2048), bf16), square]
+        + [square, square, square, square]
         + [vm((1024, 2048), bf16), vm((512, 2048), bf16), vm((512, 2048), bf16)]
         + [vm((3, 128, n), bf16) for n in widths]
         + [vm((128, n), bf16) for n in widths]
         + [vm((15, 16, n // 2), bf16) for n in widths]
         + [vm((16, n // 2), bf16) for n in widths]
-        + [dma((3,)), dma((3,)), dma((3, 3)), dma((3, 3)), dma((3, 15)), dma((3, 15))]
-        + [dma((3, 16)), dma((3, 15)), dma((3, 3)), dma((3, 3)), dma((3,)), dma((3,))]
-        + [dma((15,)), dma((15,)), dma((4,)), dma((4,)), dma((16,)), dma((15,)), dma((16,)), dma((15,)), dma((2,))],
+        + [dma((6,)), dma((6,)), dma((6, 3)), dma((6, 3)), dma((6, 15)), dma((6, 15))]
+        + [dma((6, 16)), dma((6, 15)), dma((6, 3)), dma((6, 3)), dma((6,)), dma((6,))]
+        + [dma((15,)), dma((15,)), dma((6,)), dma((6,)), dma((16,)), dma((15,)), dma((16,)), dma((15,))],
         compiler_params=pltpu.CompilerParams(collective_id=3, has_side_effects=True, vmem_limit_bytes=VMEM_MAIN),
         name="main",
-    )(*args)
-
-
-VMEM_MAIN = 58 << 20
+    )(*[pltpu.with_memory_space_constraint(arg, pltpu.HBM) for arg in args])
+
+
+VMEM_MAIN = 47 << 20
 
 
 def local(psi, region_start, region_len, fine_mask, occupation, kinetic_taps, magic_taps, external):

time: 123 us -> 115 us (0.935)
  Pallas kernels: 122 us -> 114 us
    pallas_call x1, Pallas kernels: 116 us -> 110 us  [main_step(): pl.pallas_call(functools.partial(main_kernel, scale), out_shape=(shape((1...]
    pallas_call x1, Pallas kernels: 5.75 us -> 3.89 us  [last_step(): pl.pallas_call(last_kernel, out_shape=(shape((1024, 1024)), shape((16, 16...]
where the time goes in v3:
time: 115 us; the launch traced here: 114 us
  Pallas kernels  114 us (99%)
    pallas_call x1, Pallas kernels, main_step(): pl.pallas_call(functools.partial(main_kernel, scale), out_shape=(shape((1...  110 us
    pallas_call x1, Pallas kernels, last_step(): pl.pallas_call(last_kernel, out_shape=(shape((1024, 1024)), shape((16, 16...  3.89 us

profile of v3, /device:TPU:1, one launch (start us, length us, event | category | flops | bytes accessed | tf_op | source)
XLA Modules:
  0.0 114.4 jit_solution(8622204961149111493)
XLA Ops:
  0.6 109.7 %main.1 = (f32[16,16]{1,0:T(8,128)S(1)}, bf16[1024,1024]{1,0:T(8,128)(2,1)S(1)}, bf16[1024,1024]{1,0:T(8,128)(2,1)S(1)}) custom-call(bf16[64,4,16,256]{3,2,1,0:T(8,128)(2,1)} %psi_hbm.1, s32[1024]{0:T(1024)} %start_hbm.1, s32[1024]{0:T(1024)} %len_hbm.1, s32[16,16]{1,0:T(8,128)} %fine_hbm.1, s32[1024]{0:T(1024)} %occ_hbm.1, bf16[4,4,29]{2,1,0:T(4,128)(2,1)} %bitcast.5, ...), custom_call_target="tpu_custom_call" | custom-call | tf_op jit(solution)/shard_map/main/pallas_call | solution.py:622
  110.3 3.9 %last.1 = (bf16[1024,1024]{1,0:T(8,128)(2,1)}, f32[16,16]{1,0:T(8,128)}) custom-call(bf16[1024,1024]{1,0:T(8,128)(2,1)S(1)} %get-tuple-element.7.trial, bf16[1024,1024]{1,0:T(8,128)(2,1)S(1)} %get-tuple-element.8.s_all, f32[16,16]{1,0:T(8,128)S(1)} %get-tuple-element.9.part), custom_call_target="tpu_custom_call" | custom-call | tf_op jit(solution)/shard_map/last/pallas_call | solution.py:603

commit v4 on v3

--- a/solution.py
+++ b/solution.py
@@ -428,22 +428,9 @@
     for to_z, c in spread_x + [own_x]:
         started(c, lax.div(to_z, 2) == halves[1])
 
-    density = part[...]
-    for n in range(15):
-        density_copies[n].wait_recv()
-        density = density + parts[n]
-    density_ref[...] = pltpu.roll(density, 256 - orb * 16, 1)[:, :16]
-    potential = ext_ref[...] - xc_factor * jnp.exp(jnp.log(density) * (1.0 / 3.0))
-
-    def weigh(o, _):
-        weighted[o] = (potential * values[o]).astype(bf16)
-        return 0
-
-    lax.fori_loop(0, 64, weigh, 0, unroll=4)
-
     def along(i, _):
         for e in range(4):
-            total = jnp.dot(weighted[rows_at(i, 16)].reshape(256, 256), bands[16 + e], preferred_element_type=f32)
+            total = jnp.zeros((256, 256), f32)
             for d in range(4):
                 total = total + jnp.dot(
                     masked[rows_at(i, 16), d].reshape(256, 256), bands[d * 4 + e], preferred_element_type=f32
@@ -456,6 +443,30 @@
         return 0
 
     lax.fori_loop(0, 4, along, 0)
+    density = part[...]
+    for n in range(15):
+        density_copies[n].wait_recv()
+        density = density + parts[n]
+    density_ref[...] = pltpu.roll(density, 256 - orb * 16, 1)[:, :16]
+    potential = ext_ref[...] - xc_factor * jnp.exp(jnp.log(density) * (1.0 / 3.0))
+
+    def weigh(o, _):
+        weighted[o] = (potential * values[o]).astype(bf16)
+        return 0
+
+    lax.fori_loop(0, 64, weigh, 0, unroll=4)
+
+    def adjoint(i, _):
+        for e in range(4):
+            total = jnp.dot(weighted[rows_at(i, 16)].reshape(256, 256), bands[16 + e], preferred_element_type=f32)
+            for n in range(16):
+                spots = pl.ds(pl.multiple_of((i * 16 + n) * 64 + e * 16, 16), 16)
+                wide[spots, :] += total[n * 16 : n * 16 + 16, :128]
+                spots = pl.ds(pl.multiple_of(4096 + (i * 16 + n) * 64 + e * 16, 16), 16)
+                wide[spots, :] += total[n * 16 : n * 16 + 16, 128:]
+        return 0
+
+    lax.fori_loop(0, 4, adjoint, 0)
 
     for n, h in enumerate(halves):
         lanes = pl.ds(pl.multiple_of(128 * h, 128), 128)

time: 115 us -> 115 us (level)
  no operation moved by 1% of the time
where the time goes in v4:
time: 115 us; the launch traced here: 114 us
  Pallas kernels  114 us (99%)
    pallas_call x1, Pallas kernels, main_step(): pl.pallas_call(functools.partial(main_kernel, scale), out_shape=(shape((1...  110 us
    pallas_call x1, Pallas kernels, last_step(): pl.pallas_call(last_kernel, out_shape=(shape((1024, 1024)), shape((16, 16...  3.89 us

profile of v4, /device:TPU:1, one launch (start us, length us, event | category | flops | bytes accessed | tf_op | source)
XLA Modules:
  0.0 114.4 jit_solution(14590555523054409745)
XLA Ops:
  0.6 109.7 %main.1 = (f32[16,16]{1,0:T(8,128)S(1)}, bf16[1024,1024]{1,0:T(8,128)(2,1)S(1)}, bf16[1024,1024]{1,0:T(8,128)(2,1)S(1)}) custom-call(bf16[64,4,16,256]{3,2,1,0:T(8,128)(2,1)} %psi_hbm.1, s32[1024]{0:T(1024)} %start_hbm.1, s32[1024]{0:T(1024)} %len_hbm.1, s32[16,16]{1,0:T(8,128)} %fine_hbm.1, s32[1024]{0:T(1024)} %occ_hbm.1, bf16[4,4,29]{2,1,0:T(4,128)(2,1)} %bitcast.5, ...), custom_call_target="tpu_custom_call" | custom-call | tf_op jit(solution)/shard_map/main/pallas_call | solution.py:633
  110.3 3.9 %last.1 = (bf16[1024,1024]{1,0:T(8,128)(2,1)}, f32[16,16]{1,0:T(8,128)}) custom-call(bf16[1024,1024]{1,0:T(8,128)(2,1)S(1)} %get-tuple-element.7.trial, bf16[1024,1024]{1,0:T(8,128)(2,1)S(1)} %get-tuple-element.8.s_all, f32[16,16]{1,0:T(8,128)S(1)} %get-tuple-element.9.part), custom_call_target="tpu_custom_call" | custom-call | tf_op jit(solution)/shard_map/last/pallas_call | solution.py:614
